TPU v7x, 128 devices: a whole 4x4x4 slice. The times are simulated.
128 devices in a mesh: row: 8 (over x, z_hi), col: 16 (over y, z_lo, core).
Axes of the slice: x: 4, y: 4, z: 4 (z_hi: 2, z_lo: 2; z = z_hi * 2 + z_lo), core: 2. Of those that a mesh axis runs over, the one named last changes fastest.
Arguments:
- amplitudes: float32 [12800, 12800], P('row', 'col'), may hold values from -0.0546875 to 0.0546875
- aux_left: float32 [12800, 1280], P('col'), may hold values from -12 to 12
- aux_right: float32 [12800, 1280], P('col'), may hold values from -0.3125 to 0.3125
- left_rotation: float32 [320, 320], replicated, may hold values from -0.3125 to 0.3125
- right_rotation: float32 [320, 320], replicated, may hold values from -0.3125 to 0.3125
- occ_energy: float32 [40], replicated, may hold values from -2 to -0.5
- vir_energy: float32 [320], replicated, may hold values from 0.5 to 4
Outputs:
- residual_update: float32 [320, 40, 40, 320], P('col', 'row')
All inputs are finite; a program needn't handle non-finite values.
Results may differ from a plain program's by a relative error of at most 0.00007.
Values sent between devices are 32-bit elements; how exact they have to be, the bound alone decides.
A program may use at most 192 MiB of HBM per device.

v0:
```python
import jax
import jax.numpy as jnp
from jax import lax
from jax.sharding import Mesh
from jax.sharding import PartitionSpec as P

COL = ("col_0", "col_1", "col_2")


def own_block(parts, axes, order):
    lengths = [lax.axis_size(a) for a in axes]
    parts = parts.reshape(*lengths, *parts.shape[1:])
    parts = parts.transpose(*order, *range(len(axes), parts.ndim))
    parts = parts.reshape(-1, *parts.shape[len(axes) :])
    for k in order:
        parts = lax.psum_scatter(parts, axes[k], scatter_dimension=0, tiled=True)
    return parts[0]


def split_up(x, dim, size):
    before, after = (x.shape[:dim], x.shape[dim + 1 :])
    return jnp.moveaxis(x.reshape(*before, size, -1, *after), dim, 0)


def summed_rows(x, axes, order, dim):
    size = lax.axis_size(axes)
    return own_block(split_up(x, dim, size), axes, order)


def in_one_piece(arrays, axis, split_dim, concat_dim, along):
    both = jnp.concatenate(arrays, axis=along)
    out, at, gathered = (
        lax.all_to_all(both, axis, split_axis=split_dim, concat_axis=concat_dim, tiled=True),
        0,
        [],
    )
    for a in arrays:
        gathered.append(lax.slice_in_dim(out, at, at + a.shape[along], axis=along))
        at += a.shape[along]
    return tuple(gathered)


def piece_ends(length, count):
    unit = 8 if length >= 8 * count else 1
    return [length // unit * k // count * unit for k in range(1, count)]


def in_order(parts, dim):
    lengths = list(parts.shape[1:])
    lengths[dim] *= parts.shape[0]
    return jnp.moveaxis(parts, 0, dim).reshape(lengths)


def cut_exchange(x, axis, pieces, split_dim, concat_dim):
    parts = split_up(x, split_dim, lax.axis_size(axis))
    cut = max(range(1, max(2, parts.ndim - 1)), key=lambda d: parts.shape[d])
    gathered = []
    for section in jnp.split(parts, piece_ends(parts.shape[cut], pieces), axis=cut):
        if section.size:
            gathered.append(lax.all_to_all(section, axis, split_axis=0, concat_axis=0, tiled=True))
    return in_order(jnp.concatenate(gathered, axis=cut), concat_dim)


def shards(amplitudes, aux_left, aux_right, left_rotation, right_rotation, occ_energy, vir_energy):
    highest = lax.Precision.HIGHEST
    n_row = lax.axis_size("row")
    rows_local, cols_local = amplitudes.shape
    occ_count = occ_energy.shape[0]
    vir_count = vir_energy.shape[0]
    vir_rows = rows_local // occ_count
    vir_cols = cols_local // occ_count
    occ_group = occ_count // n_row
    columns = aux_left
    shared = summed_rows(
        lax.dot_general(
            columns,
            amplitudes,
            (((0,), (1,)), ((), ())),
            precision=highest,
            preferred_element_type=jnp.float32,
        ),
        COL,
        (2, 0, 1),
        0,
    )
    columns = aux_right
    paired = lax.dot_general(
        lax.all_gather(shared, COL, axis=0, tiled=True),
        columns,
        (((0,), (1,)), ((), ())),
        precision=highest,
        preferred_element_type=jnp.float32,
    )
    direct = paired.reshape(vir_rows, occ_count, cols_local)
    mirror = (
        paired.reshape(vir_rows, occ_count, vir_cols, occ_count)
        .transpose(0, 3, 2, 1)
        .reshape(vir_rows, occ_count, cols_local)
    )
    direct, mirror = in_one_piece((direct, mirror), "row", 1, 0, 2)
    mirror = cut_exchange(mirror, COL, 2, 0, 2)
    mirror_four = mirror.reshape(vir_cols, occ_group, vir_count, occ_count)
    summed = direct.reshape(vir_count, occ_group, vir_cols, occ_count) + mirror_four.transpose(
        2, 1, 0, 3
    )
    half_rot = jnp.dot(
        left_rotation,
        summed.reshape(vir_count, occ_group * cols_local),
        precision=highest,
        preferred_element_type=jnp.float32,
    )
    half_rot = cut_exchange(half_rot.reshape(vir_count, occ_group, cols_local), COL, 2, 0, 2)
    rotated = jnp.einsum(
        "aibj,Bb->aijB",
        half_rot.reshape(vir_cols, occ_group, vir_count, occ_count),
        right_rotation,
        precision=highest,
    )
    vir_here = lax.dynamic_slice_in_dim(vir_energy, lax.axis_index(COL) * vir_cols, vir_cols)
    occ_here = lax.dynamic_slice_in_dim(occ_energy, lax.axis_index("row") * occ_group, occ_group)
    denominator = (
        vir_here[:, None, None, None]
        + vir_energy[None, None, None, :]
        - occ_here[None, :, None, None]
        - occ_energy[None, None, :, None]
    )
    return rotated / denominator


def solution(mesh):
    finer = Mesh(
        mesh.devices.reshape(mesh.shape["row"], 4, 2, 2), ("row", "col_0", "col_1", "col_2")
    )
    placed = (P("row", COL), P(COL, None), P(COL, None), P(), P(), P(), P())
    return jax.shard_map(
        shards, mesh=finer, in_specs=placed, out_specs=P(COL, "row", None, None), check_vma=False
    )
```

profile of v0, /device:TPU:48, one launch (start us, length us, event | category | flops | bytes accessed | tf_op | source)
XLA Modules:
  0.0 795.7 jit_solution(11221773862076111729)
XLA Ops:
  6.5 36.2 %fusion.4 = f32[1280,1600]{1,0:T(8,128)S(1)} fusion(f32[800,1280]{1,0:T(8,128)} %param.8, f32[1600,800]{0,1:T(8,128)} %param.7), kind=kOutput, calls=%fused_computation.13 | convolution fusion | flops 19660800000 | bytes 17408000 | tf_op jit(solution)/shard_map/dot_general | solution.py:75
  42.8 4.0 copy.32
  46.8 21.7 %reduce-scatter.4.cloned.1.call-done = f32[8,80,1600]{2,1,0:T(8,128)} async-done(((f32[16,80,1600]{2,1,0:T(8,128)}), f32[8,80,1600]{2,1,0:T(8,128)}) %reduce-scatter.4.cloned.1.call-update) | async-done | bytes 4096016 | tf_op jit(solution)/shard_map/reduce_scatter | solution.py:16
  68.6 49.6 %reduce-scatter.6.cloned.1.call-done = f32[2,80,1600]{2,1,0:T(8,128)} async-done(((f32[8,80,1600]{2,1,0:T(8,128)}), f32[2,80,1600]{2,1,0:T(8,128)}) %reduce-scatter.6.cloned.1.call-update) | async-done | bytes 1024016 | tf_op jit(solution)/shard_map/reduce_scatter | solution.py:16
  118.2 25.6 %reduce-scatter.8.cloned.1.call-done = f32[1,80,1600]{2,1,0:T(8,128)} async-done(((f32[2,80,1600]{2,1,0:T(8,128)}), f32[1,80,1600]{2,1,0:T(8,128)}) %reduce-scatter.8.cloned.1.call-update) | async-done | bytes 512016 | tf_op jit(solution)/shard_map/reduce_scatter | solution.py:16
  143.8 56.1 %all-gather.3.cloned.1.call-done = f32[1,1280,1600]{2,1,0:T(8,128)} async-done(((f32[1,80,1600]{2,1,0:T(8,128)}), f32[1,1280,1600]{2,1,0:T(8,128)}) %all-gather.3.cloned.1.call-update) | async-done | bytes 8192016 | tf_op jit(solution)/shard_map/all_gather | solution.py:88
  200.0 27.0 %fusion = f32[1600,800]{0,1:T(8,128)} fusion(f32[800,1280]{1,0:T(8,128)} %param.9, f32[1,1280,1600]{2,1,0:T(8,128)} %all-gather.3.cloned.1.call-done), kind=kOutput, calls=%fused_computation.2 | convolution fusion | flops 19660800000 | bytes 17408000 | tf_op jit(solution)/shard_map/dot_general | solution.py:87
  227.0 12.6 %reshape.59 = f32[40,40,20,40]{1,0,3,2:T(8,128)} reshape(f32[1600,800]{0,1:T(8,128)} %fusion) | data formatting | bytes 10240000 | tf_op jit(solution)/shard_map/reshape | solution.py:96
  239.6 6.8 copy.33
  246.4 18.6 %copy.50 = f32[40,40,20,40]{1,2,3,0:T(8,128)} copy(f32[40,40,20,40]{1,0,3,2:T(8,128)} %reshape.59) | data formatting | bytes 10240000 | tf_op jit(solution)/shard_map/reshape | solution.py:96
  265.0 14.3 %reshape.60 = f32[40,40,800]{2,1,0:T(8,128)} reshape(f32[40,40,20,40]{3,2,1,0:T(8,128)} %bitcast.44) | data formatting | bytes 10240000 | tf_op jit(solution)/shard_map/reshape | solution.py:98
  279.4 10.2 %pad_maximum_fusion = f32[40,40,1600]{2,1,0:T(8,128)} fusion(f32[40,40,800]{2,1,0:T(8,128)} %reshape.60, f32[40,40,800]{2,1,0:T(8,128)} %bitcast.50), kind=kLoop, calls=%fused_computation.1 | loop fusion | flops 2560000 | bytes 20480000 | tf_op jit(solution)/shard_map/concatenate | solution.py:31
  289.5 6.1 copy.35
  295.6 126.3 %all_to_all.38 = f32[40,40,1600]{2,0,1:T(8,128)} all-to-all(f32[40,40,1600]{2,0,1:T(8,128)S(1)} %copy.35), channel_id=1, replica_groups=mesh['row'=8,'col_0'=4,'col_1'=2,'col_2'=2] {'row'}, dimensions={1} | all-to-all | bytes 20480000 | tf_op jit(solution)/shard_map/all_to_all | solution.py:33
  421.9 4.7 copy.36
  426.7 6.2 fusion.3
  432.8 7.0 reshape.62
  439.8 1.6 slice-done.2
  441.4 1.5 copy.38
  443.0 5.7 all-to-all-start.1
  448.7 2.3 slice-done.3
  451.0 2.4 copy.39
  453.4 24.9 %all-to-all-done.1 = f32[16,8,5,800]{3,1,2,0:T(8,128)S(1)} async-done(((f32[16,8,5,800]{3,1,2,0:T(8,128)}), f32[16,8,5,800]{3,1,2,0:T(8,128)S(1)}, u32[]{:S(2)}, u32[]{:S(2)}) %all-to-all-start.1) | async-done | bytes 2048032 | tf_op jit(solution)/shard_map/all_to_all | solution.py:60
  478.2 5.7 all-to-all-start.2
  484.0 7.7 copy.37
  491.7 57.4 %all-to-all-done.2 = f32[16,12,5,800]{3,1,2,0:T(8,128)} async-done(((f32[16,12,5,800]{3,1,2,0:T(8,128)}), f32[16,12,5,800]{3,1,2,0:T(8,128)}, u32[]{:S(2)}, u32[]{:S(2)}) %all-to-all-start.2) | async-done | bytes 3072032 | tf_op jit(solution)/shard_map/all_to_all | solution.py:60
  549.1 2.8 maximum_bitcast_fusion
  551.8 3.5 copy.40
  555.3 12.8 %reshape_reshape.13 = f32[20,5,320,40]{3,2,1,0:T(8,128)} reshape(f32[20,5,16,800]{3,2,1,0:T(8,128)} %copy.40) | data formatting | bytes 10240000 | tf_op jit(solution)/shard_map/reshape;reshape | solution.py:102
  568.1 12.7 %copy.41 = f32[20,5,320,40]{2,3,0,1:T(8,128)} copy(f32[20,5,320,40]{3,2,1,0:T(8,128)} %reshape_reshape.13) | data formatting | bytes 10240000 | tf_op jit(solution)/shard_map/reshape;reshape | solution.py:102
  580.8 5.1 bitcast_add_fusion
  585.9 10.2 %convolution_bitcast_fusion = f32[320,4000]{1,0:T(8,128)} fusion(f32[320,4000]{0,1:T(8,128)S(1)} %bitcast.46, f32[320,320]{1,0:T(8,128)S(1)} %copy-done), kind=kOutput, calls=%fused_computation.8 | convolution fusion | flops 4915200000 | bytes 10649600 | tf_op jit(solution)/shard_map/dot_general | solution.py:106
  596.2 8.7 %reshape_reshape.14 = f32[16,20,5,800]{3,2,1,0:T(8,128)} reshape(f32[320,4000]{1,0:T(8,128)} %convolution_bitcast_fusion) | data formatting | bytes 10240000 | tf_op jit(solution)/shard_map/reshape;reshape | solution.py:22
  604.9 2.0 slice-done
  606.9 1.8 copy.42
  608.7 5.7 all-to-all-start.3
  614.4 2.6 slice-done.1
  616.9 2.8 copy.43
  619.8 24.1 %all-to-all-done.3 = f32[16,8,5,800]{3,1,2,0:T(8,128)S(1)} async-done(((f32[16,8,5,800]{3,1,2,0:T(8,128)}), f32[16,8,5,800]{3,1,2,0:T(8,128)S(1)}, u32[]{:S(2)}, u32[]{:S(2)}) %all-to-all-start.3) | async-done | bytes 2048032 | tf_op jit(solution)/shard_map/all_to_all | solution.py:60
  643.9 6.1 all-to-all-start.4
  650.0 0.1 dynamic_slice.6
  650.1 0.1 dynamic_slice.7
  650.2 0.1 broadcast_subtract_fusion
  650.3 64.3 %all-to-all-done.4 = f32[16,12,5,800]{3,1,2,0:T(8,128)} async-done(((f32[16,12,5,800]{3,1,2,0:T(8,128)}), f32[16,12,5,800]{3,1,2,0:T(8,128)}, u32[]{:S(2)}, u32[]{:S(2)}) %all-to-all-start.4) | async-done | bytes 3072032 | tf_op jit(solution)/shard_map/all_to_all | solution.py:60
  714.7 2.8 maximum_bitcast_fusion.1
  717.4 3.6 copy.44
  721.0 12.8 %reshape_reshape.15 = f32[20,5,320,40]{3,2,1,0:T(8,128)} reshape(f32[20,5,16,800]{3,2,1,0:T(8,128)} %copy.44) | data formatting | bytes 10240000 | tf_op jit(solution)/shard_map/reshape;reshape | solution.py:115
  733.8 55.0 %subtract_divide_fusion = f32[20,5,40,320]{3,2,1,0:T(8,128)} fusion(f32[40]{0:T(128)S(1)} %copy-done.3, f32[20,5,320]{2,1,0:T(8,128)S(1)} %broadcast_subtract_fusion, f32[20,5,320,40]{3,2,1,0:T(8,128)} %reshape_reshape.15, f32[320,320]{1,0:T(8,128)S(1)} %copy-done.2), kind=kOutput, calls=%fused_computation.7 | convolution fusion | flops 4917760000 | bytes 10777760 | tf_op jit(solution)/shard_map/aibj,Bb->aijB/dot_general | solution.py:113
  (21 shorter events, 0.3 us)
Async XLA Ops:
  6.5 579.4 %copy-start = (f32[320,320]{1,0:T(8,128)S(1)}, f32[320,320]{1,0:T(8,128)}, u32[]{:S(2)}) copy-start(f32[320,320]{1,0:T(8,128)} %param.10) | copy-start | bytes 1228804
  6.5 62.0 %reduce-scatter.4.cloned.1.call-start = ((), (), s32[]{:S(2)}) async-start(), calls=%async_computation.8 | async-start | bytes 12779520 | tf_op jit(solution)/shard_map/reduce_scatter | solution.py:16
  46.8 71.4 %reduce-scatter.6.cloned.1.call-start = ((), (), s32[]{:S(2)}) async-start(), calls=%async_computation.9 | async-start | bytes 5324800 | tf_op jit(solution)/shard_map/reduce_scatter | solution.py:16
  68.5 75.3 %reduce-scatter.8.cloned.1.call-start = ((), (), s32[]{:S(2)}) async-start(), calls=%async_computation.10 | async-start | bytes 1597440 | tf_op jit(solution)/shard_map/reduce_scatter | solution.py:16
  118.2 81.8 %all-gather.3.cloned.1.call-start = ((), (), s32[]{:S(2)}) async-start(), calls=%async_computation.11 | async-start | bytes 9052160 | tf_op jit(solution)/shard_map/all_gather | solution.py:88
  439.8 1.6 slice-start.2
  443.0 35.3 %all-to-all-start.1 = ((f32[16,8,5,800]{3,1,2,0:T(8,128)}), f32[16,8,5,800]{3,1,2,0:T(8,128)S(1)}, u32[]{:S(2)}, u32[]{:S(2)}) async-start(f32[16,8,5,800]{3,1,2,0:T(8,128)} %copy.38), calls=%async_computation.4 | async-start | bytes 4587520 | tf_op jit(solution)/shard_map/all_to_all | solution.py:60
  448.7 2.3 slice-start.3
  478.2 70.8 %all-to-all-start.2 = ((f32[16,12,5,800]{3,1,2,0:T(8,128)}), f32[16,12,5,800]{3,1,2,0:T(8,128)}, u32[]{:S(2)}, u32[]{:S(2)}) async-start(f32[16,12,5,800]{3,1,2,0:T(8,128)} %copy.39), calls=%async_computation.5 | async-start | bytes 9175040 | tf_op jit(solution)/shard_map/all_to_all | solution.py:60
  604.8 2.0 slice-start
  608.7 35.3 %all-to-all-start.3 = ((f32[16,8,5,800]{3,1,2,0:T(8,128)}), f32[16,8,5,800]{3,1,2,0:T(8,128)S(1)}, u32[]{:S(2)}, u32[]{:S(2)}) async-start(f32[16,8,5,800]{3,1,2,0:T(8,128)} %copy.42), calls=%async_computation.6 | async-start | bytes 4587520 | tf_op jit(solution)/shard_map/all_to_all | solution.py:60
  614.4 2.6 slice-start.1
  619.8 30.2 %copy-start.1 = (f32[320]{0:T(512)S(1)}, f32[320]{0:T(512)}, u32[]{:S(2)}) copy-start(f32[320]{0:T(512)} %param.13) | copy-start | bytes 3844
  619.8 30.3 %copy-start.3 = (f32[40]{0:T(128)S(1)}, f32[40]{0:T(128)}, u32[]{:S(2)}) copy-start(f32[40]{0:T(128)} %param.12) | copy-start | bytes 484
  643.9 70.7 %all-to-all-start.4 = ((f32[16,12,5,800]{3,1,2,0:T(8,128)}), f32[16,12,5,800]{3,1,2,0:T(8,128)}, u32[]{:S(2)}, u32[]{:S(2)}) async-start(f32[16,12,5,800]{3,1,2,0:T(8,128)} %copy.43), calls=%async_computation.7 | async-start | bytes 9175040 | tf_op jit(solution)/shard_map/all_to_all | solution.py:60
  721.0 12.8 %copy-start.2 = (f32[320,320]{1,0:T(8,128)S(1)}, f32[320,320]{1,0:T(8,128)}, u32[]{:S(2)}) copy-start(f32[320,320]{1,0:T(8,128)} %param.11) | copy-start | bytes 1228804
Sparse Core Ops, SparseCore 0:
  46.9 21.5 reduce-scatter.3
  71.1 47.0 reduce-scatter.5
  120.5 23.2 reduce-scatter.7
  145.5 54.4 all-gather.2
where the time goes:
time: 809 us; the launch traced here: 796 us
  waiting for transfers between devices  324 us (40%)
  local copies, waits for them, and re-layouts  159 us (20%)
  matrix products  128 us (16%)
  blocking collectives  126 us (16%)
  starting transfers between devices  23.4 us (3%)
  other arithmetic  21 us (3%)
  between operations  13.6 us (2%)
    all_to_all x4, waiting for transfers between devices, cut_exchange(): lax.all_to_all(section, axis, split_axis=0, concat_axis=0, tiled=True)  171 us
    all_to_all x1, blocking collectives, in_one_piece(): lax.all_to_all(both, axis, split_axis=split_dim, concat_axis=concat_dim,...  126 us
    reduce_scatter x3, waiting for transfers between devices, own_block(): parts = lax.psum_scatter(parts, axes[k], scatter_dimension=0, tiled=True)  96.9 us
    all_gather x1, waiting for transfers between devices, shards(): lax.all_gather(shared, COL, axis=0, tiled=True)  56.1 us
    dot_general x1, matrix products, shards(): jnp.einsum('aibj,Bb->aijB', half_rot.reshape(vir_cols, occ_group, vir_cou...  55 us
    dot_general x1, matrix products, shards(): lax.dot_general(columns, amplitudes, (((0,), (1,)), ((), ())), precision=...  36.2 us
    reshape x2, local copies, waits for them, and re-layouts, shards(): paired.reshape(vir_rows, occ_count, vir_cols, occ_count)  31.2 us
    dot_general x1, matrix products, shards(): lax.dot_general(lax.all_gather(shared, COL, axis=0, tiled=True), columns,...  27 us
  transfers between devices with their start and end apart: 8, of which 8 were waited for; matrix products, arithmetic and copies ran while one was open for 2% of the time, Pallas kernels for 0%

commit v1 on v0

v1 whole, which is shorter than its diff:
```python
import functools

import jax
import jax.numpy as jnp
from jax import lax
from jax.experimental import pallas as pl
from jax.experimental.pallas import tpu as pltpu
from jax.sharding import PartitionSpec as P

MESH = pl.DeviceIdType.MESH
F32 = jnp.float32
BF16 = jnp.bfloat16
WIDE = 256


def halves(x):
    hi = x.astype(BF16)
    return hi, (x - hi.astype(F32)).astype(BF16)


def dot3(xh, xl, yh, yl, dims):
    def dot(a, b):
        return lax.dot_general(a, b, (dims, ((), ())), preferred_element_type=F32)

    return dot(xl, yh) + dot(xh, yl) + dot(xh, yh)


def up(n, unit):
    return -(-n // unit) * unit


def planes(src, dst):
    width, rows = src.shape[1], 40 if src.shape[0] % 40 == 0 else src.shape[0]

    def one(g, _):
        at = pl.ds(pl.multiple_of(g * rows, 8), rows)
        for p in range(dst.shape[0]):
            n = min(128, width - p * 128)
            dst[p, at, :n] = src[at, p * 128 : p * 128 + n]
        return 0

    lax.fori_loop(0, src.shape[0] // rows, one, 0)


def every(src, start, count, stride, width):
    parts = [src[p, pl.ds(start, count, stride=stride), :] for p in range(src.shape[0])]
    return jnp.concatenate(parts, axis=1)[:, :width]


def gather_kernel(
    nr, occ,
    t_ref, b_ref, z_ref,
    fg_ref, zg_ref,
    tp, zp, bh, bl, sib_send, sib_recv, own, rs_recv, fp, zs_send, zs_recv, zc,
    sib_s, sib_r, rs_s, rs_r, zs_s, zs_r, za_s, za_r, fa_s, fa_r, loc,
):
    r, c = lax.axis_index("row"), lax.axis_index("col")
    t, k = c // 2, lax.rem(c, 2)
    sib = c + 1 - 2 * k
    og = occ // nr
    va = t_ref.shape[0] // occ
    vc = z_ref.shape[0] // occ
    half = b_ref.shape[1] // 2
    blk = lax.rem(t - r + nr, nr)
    is_own = lax.rem(r + r, nr) == t

    barrier = pltpu.get_barrier_semaphore()
    pl.semaphore_signal(barrier, inc=1, device_id=(r, sib), device_id_type=MESH)

    def greet(s, _):
        peer = lax.rem(t + 1 + s, nr)
        pl.semaphore_signal(barrier, inc=1, device_id=(r, 2 * peer + k), device_id_type=MESH)
        return 0

    lax.fori_loop(0, nr - 1, greet, 0)

    def greet_sources(s, _):
        @pl.when(jnp.logical_not(jnp.logical_and(is_own, s == t)))
        def _():
            pl.semaphore_signal(barrier, inc=1, device_id=(blk, 2 * s + k), device_id_type=MESH)

        return 0

    lax.fori_loop(0, nr, greet_sources, 0)

    planes(t_ref, tp)
    planes(z_ref, zp)
    mine, other = pl.ds(pl.multiple_of(k * half, half), half), pl.ds(pl.multiple_of((1 - k) * half, half), half)
    for at, cols in ((0, other), (half, mine)):
        hi, lo = halves(b_ref[:, cols])
        bh[:, at : at + half] = hi
        bl[:, at : at + half] = lo

    first = k == 0
    kept = []
    for jj in range(og):
        z = every(zp, r * og + jj, vc, occ, z_ref.shape[1])
        z0, z1 = z[:, :half], z[:, half:]
        zs_send[jj] = jnp.where(first, z1, z0)
        kept.append(jnp.where(first, z0, z1))
        zc[jj * va : jj * va + vc, :] = kept[-1]

    @pl.when(is_own)
    def _():
        pl.semaphore_wait(barrier, 2 * nr - 1)

    @pl.when(jnp.logical_not(is_own))
    def _():
        pl.semaphore_wait(barrier, 2 * nr)

    z_swap = pltpu.make_async_remote_copy(
        src_ref=zs_send, dst_ref=zs_recv, send_sem=zs_s, recv_sem=zs_r,
        device_id=(r, sib), device_id_type=MESH,
    )
    z_swap.start()
    z_swap.wait()
    for jj in range(og):
        z_mine = zc[jj * va : jj * va + vc, :]
        z_sib = zs_recv[jj]
        zc[jj * va : (jj + 1) * va, :] = jnp.concatenate(
            [jnp.where(first, z_mine, z_sib), jnp.where(first, z_sib, z_mine)], axis=0
        )

    def spread(src, dst, slot, send, recv, s):
        peer = lax.rem(t + 1 + s, nr)
        return pltpu.make_async_remote_copy(
            src_ref=src, dst_ref=dst.at[slot], send_sem=send.at[s], recv_sem=recv.at[slot],
            device_id=(r, 2 * peer + k), device_id_type=MESH,
        )

    def z_start(s, _):
        spread(zc, zg_ref, t, za_s, za_r, s).start()
        return 0

    lax.fori_loop(0, nr - 1, z_start, 0)
    z_own = pltpu.make_async_copy(zc, zg_ref.at[t], loc.at[0])
    z_own.start()

    def to_sibling(s):
        return pltpu.make_async_remote_copy(
            src_ref=sib_send.at[s], dst_ref=sib_recv.at[s], send_sem=sib_s.at[s], recv_sem=sib_r.at[s],
            device_id=(r, sib), device_id_type=MESH,
        )

    def to_owner(s):
        dst = lax.rem(r + 1 + s, nr)
        return pltpu.make_async_remote_copy(
            src_ref=own.at[s], dst_ref=rs_recv.at[t], send_sem=rs_s.at[s], recv_sem=rs_r.at[t],
            device_id=(dst, 2 * lax.rem(r + dst, nr) + k), device_id_type=MESH,
        )

    last_is_own = is_own

    def finish(s):
        to_sibling(s).wait_recv()
        own[s] = own[s] + sib_recv[s]
        here = jnp.logical_and(s == nr - 1, last_is_own)

        @pl.when(here)
        def _():
            rs_recv[t] = own[s]

        @pl.when(jnp.logical_not(here))
        def _():
            to_owner(s).start()

    def step(s, _):
        dst = lax.rem(r + 1 + s, nr)
        x = jnp.concatenate(
            [every(tp, dst * og + ii, va, occ, t_ref.shape[1]) for ii in range(og)], axis=0
        )
        xh, xl = halves(x)
        part = dot3(xh, xl, bh[...], bl[...], ((1,), (0,)))
        sib_send[s] = part[:, :half]
        own[s] = part[:, half:]
        to_sibling(s).start()

        @pl.when(s > 0)
        def _():
            finish(s - 1)

        return 0

    lax.fori_loop(0, nr, step, 0)
    finish(nr - 1)

    def arrived(s, _):
        @pl.when(jnp.logical_not(jnp.logical_and(is_own, s == t)))
        def _():
            pltpu.make_async_remote_copy(
                src_ref=own.at[0], dst_ref=rs_recv.at[s], send_sem=rs_s.at[0], recv_sem=rs_r.at[s],
                device_id=(r, sib), device_id_type=MESH,
            ).wait_recv()

        return 0

    lax.fori_loop(0, nr, arrived, 0)

    def add_up(g, _):
        rows = pl.ds(pl.multiple_of(g * 8, 8), 8)
        total = rs_recv[0, rows, :]
        for s in range(1, nr):
            total = total + rs_recv[s, rows, :]
        fp[rows, :] = total
        return 0

    lax.fori_loop(0, fp.shape[0] // 8, add_up, 0)

    def f_start(s, _):
        spread(fp, fg_ref, blk, fa_s, fa_r, s).start()
        return 0

    lax.fori_loop(0, nr - 1, f_start, 0)
    f_own = pltpu.make_async_copy(fp, fg_ref.at[blk], loc.at[1])
    f_own.start()

    def settle(s, _):
        peer = lax.rem(t + 1 + s, nr)
        spread(zc, zg_ref, peer, za_s, za_r, s).wait()
        spread(fp, fg_ref, lax.rem(peer - r + nr, nr), fa_s, fa_r, s).wait()
        return 0

    lax.fori_loop(0, nr - 1, settle, 0)

    def sent(s, _):
        to_sibling(s).wait_send()

        @pl.when(jnp.logical_not(jnp.logical_and(s == nr - 1, last_is_own)))
        def _():
            to_owner(s).wait_send()

        return 0

    lax.fori_loop(0, nr, sent, 0)
    z_own.wait()
    f_own.wait()


def tile_kernel(
    nr, og, vc, tiles,
    fg_ref, zg_ref, l_ref, r_ref, rowd_ref, cold_ref,
    out_ref,
    rh, rl, yh, yl, xp, xo, xg, xh, xl, s_send, s_recv, own,
    xs, xr, ss, sr, os_, or_, loc,
):
    r, c = lax.axis_index("row"), lax.axis_index("col")
    t, k = c // 2, lax.rem(c, 2)
    sib = c + 1 - 2 * k
    half = fg_ref.shape[2]
    vir = r_ref.shape[0]
    va = vir // nr
    pad = xo.shape[1] // 2
    wide_pad = xh.shape[1] // nr

    barrier = pltpu.get_barrier_semaphore()
    pl.semaphore_signal(barrier, inc=1, device_id=(r, sib), device_id_type=MESH)

    def greet(s, _):
        pl.semaphore_signal(barrier, inc=1, device_id=(lax.rem(r + 1 + s, nr), c), device_id_type=MESH)
        return 0

    lax.fori_loop(0, nr - 1, greet, 0)

    hi, lo = halves(r_ref[...])
    rh[...] = hi
    rl[...] = lo
    lh, ll = halves(l_ref[pl.ds(pl.multiple_of(t * va, 8), va), :])
    xp[...] = jnp.zeros_like(xp)
    pl.semaphore_wait(barrier, nr)

    def x_copy(q, s):
        return pltpu.make_async_remote_copy(
            src_ref=xo.at[q], dst_ref=xg.at[r, q], send_sem=xs.at[q, s], recv_sem=xr.at[q, r],
            device_id=(lax.rem(r + 1 + s, nr), c), device_id_type=MESH,
        )

    def x_wait(q, s):
        src = lax.rem(r + 1 + s, nr)
        return pltpu.make_async_remote_copy(
            src_ref=xo.at[q], dst_ref=xg.at[src, q], send_sem=xs.at[q, s], recv_sem=xr.at[q, src],
            device_id=(src, c), device_id_type=MESH,
        )

    for q, g_ref in ((1, zg_ref), (0, fg_ref)):
        y_at = (1 - q) * half
        for ii in range(og):
            gh, gl = halves(g_ref[:, ii * va : (ii + 1) * va, :].reshape(vir, half))
            x = dot3(lh, ll, gh, gl, ((1,), (0,)))
            for par in range(2):
                for p in range(half // 128):
                    xp[p, pl.ds(par * pad + ii, vc, stride=og), :] = x[
                        par * vc : (par + 1) * vc, p * 128 : (p + 1) * 128
                    ]
            y = dot3(rh[...], rl[...], gh, gl, ((1,), (0,)))
            hi, lo = halves(y)
            yh[ii * vir : (ii + 1) * vir, y_at : y_at + half] = hi
            yl[ii * vir : (ii + 1) * vir, y_at : y_at + half] = lo

        for p in range(half // 128):
            xo[q, :, p * 128 : (p + 1) * 128] = xp[p]

        def x_start(s, _, q=q):
            x_copy(q, s).start()
            return 0

        lax.fori_loop(0, nr - 1, x_start, 0)

    def take(src, q, load):
        x_at = q * half
        at = pl.multiple_of(src * wide_pad, 16)
        for par in range(2):
            hi, lo = halves(load(par))
            xh[par, pl.ds(at, pad), x_at : x_at + half] = hi
            xl[par, pl.ds(at, pad), x_at : x_at + half] = lo

    for q in (1, 0):
        take(r, q, lambda par, q=q: xo[q, par * pad : (par + 1) * pad, :])

        def x_take(s, _, q=q):
            src = lax.rem(r + 1 + s, nr)
            x_wait(q, s).wait_recv()
            take(src, q, lambda par: xg[src, q, par * pad : (par + 1) * pad, :])
            return 0

        lax.fori_loop(0, nr - 1, x_take, 0)

    def to_sibling(n, width):
        return pltpu.make_async_remote_copy(
            src_ref=s_send.at[lax.rem(n, 2), :, pl.ds(0, width)], dst_ref=s_recv.at[n, :, pl.ds(0, width)],
            send_sem=ss.at[lax.rem(n, 2)], recv_sem=sr.at[n],
            device_id=(r, sib), device_id_type=MESH,
        )

    def to_row(n, width, s, src):
        dst = lax.rem(r + 1 + s, nr)
        cols = pl.ds(pl.multiple_of(n * WIDE, 128), width)
        return pltpu.make_async_remote_copy(
            src_ref=own.at[pl.ds(pl.multiple_of(dst * wide_pad, 8), pad), cols],
            dst_ref=out_ref.at[src, :, cols],
            send_sem=os_.at[n, s], recv_sem=or_.at[n, src],
            device_id=(dst, c), device_id_type=MESH,
        )

    def stay(n, width):
        cols = pl.ds(pl.multiple_of(n * WIDE, 128), width)
        return pltpu.make_async_copy(
            own.at[pl.ds(pl.multiple_of(r * wide_pad, 8), pad), cols], out_ref.at[r, :, cols], loc.at[n]
        )

    def tile(n, width, slot_used):
        rows = pl.ds(pl.multiple_of(n * WIDE, 128), width)
        wh, wl = yh[rows, :], yl[rows, :]

        def product(par):
            return dot3(xh[par], xl[par], wh, wl, ((1,), (1,)))

        @pl.when(slot_used)
        def _():
            to_sibling(n - 2, WIDE).wait_send()

        s_send[lax.rem(n, 2), :, 0:width] = product(1 - k)
        to_sibling(n, width).start()
        own[:, rows] = product(k)
        to_sibling(n, width).wait_recv()
        reps = width // 128

        def close(g, _):
            at = pl.ds(pl.multiple_of(g * 8, 8), 8)
            rowd = rowd_ref[at, :]
            for m in range(reps):
                cols = pl.ds(pl.multiple_of(n * WIDE + m * 128, 128), 128)
                here = own[at, cols] + s_recv[n, at, m * 128 : (m + 1) * 128]
                own[at, cols] = here / (rowd + cold_ref[:, cols])
            return 0

        lax.fori_loop(0, own.shape[0] // 8, close, 0)

        def send(s, _):
            to_row(n, width, s, r).start()
            return 0

        lax.fori_loop(0, nr - 1, send, 0)
        stay(n, width).start()

    tail = yh.shape[0] - (tiles - 1) * WIDE

    def full(n, _):
        tile(n, WIDE, n > 1)
        return 0

    lax.fori_loop(0, tiles - 1, full, 0)
    tile(jnp.int32(tiles - 1), tail, tiles > 2)

    def settle(n, width):
        def one(s, _):
            src = lax.rem(r + 1 + s, nr)
            to_row(n, width, s, src).wait()
            return 0

        lax.fori_loop(0, nr - 1, one, 0)
        stay(n, width).wait()

    def settle_full(n, _):
        settle(n, WIDE)
        return 0

    lax.fori_loop(0, tiles - 1, settle_full, 0)
    settle(jnp.int32(tiles - 1), tail)
    to_sibling(jnp.int32(tiles - 2), WIDE).wait_send()
    to_sibling(jnp.int32(tiles - 1), tail).wait_send()
    for q in (1, 0):
        def x_sent(s, _, q=q):
            x_copy(q, s).wait_send()
            return 0

        lax.fori_loop(0, nr - 1, x_sent, 0)


def lay_kernel(nr, og, vir, occ, in_ref, out_ref, op):
    count, wide = op.shape[0], in_ref.shape[2]
    for src in range(nr):
        for jj in range(og):
            for p in range(count):
                start = jj * vir + p * 128
                n = min(128, wide - start)
                v = in_ref[src, :, start : start + n]
                if n < 128:
                    v = jnp.concatenate([v, jnp.zeros((8, 128 - n), F32)], axis=1)
                op[p, pl.ds(src * og + jj, 8, stride=occ), :] = v
    for p in range(count):
        n = min(128, vir - p * 128)
        out_ref[:, p * 128 : p * 128 + n] = op[p, :, :n]


def shards(amplitudes, aux_left, aux_right, left_rotation, right_rotation, occ_energy, vir_energy):
    nr, nc = lax.axis_size("row"), lax.axis_size("col")
    occ, vir = occ_energy.shape[0], vir_energy.shape[0]
    naux = aux_left.shape[1]
    half = naux // 2
    og, va, vc = occ // nr, vir // nr, vir // nc
    piece = og * va
    dma = pltpu.SemaphoreType.DMA
    vmem = pl.BlockSpec(memory_space=pltpu.VMEM)
    hbm = pl.BlockSpec(memory_space=pl.ANY)
    limit = 60 * 1024 * 1024

    fg, zg = pl.pallas_call(
        functools.partial(gather_kernel, nr, occ),
        out_shape=[jax.ShapeDtypeStruct((nr, piece, half), F32)] * 2,
        in_specs=[vmem] * 3,
        out_specs=[hbm] * 2,
        scratch_shapes=[
            pltpu.VMEM((up(amplitudes.shape[1], 128) // 128, amplitudes.shape[0], 128), F32),
            pltpu.VMEM((up(naux, 128) // 128, aux_right.shape[0], 128), F32),
            pltpu.VMEM((aux_left.shape[0], naux), BF16),
            pltpu.VMEM((aux_left.shape[0], naux), BF16),
            pltpu.VMEM((nr, piece, half), F32),
            pltpu.VMEM((nr, piece, half), F32),
            pltpu.VMEM((nr, piece, half), F32),
            pltpu.VMEM((nr, piece, half), F32),
            pltpu.VMEM((piece, half), F32),
            pltpu.VMEM((og, vc, half), F32),
            pltpu.VMEM((og, vc, half), F32),
            pltpu.VMEM((piece, half), F32),
            dma((nr,)), dma((nr,)), dma((nr,)), dma((nr,)), dma, dma,
            dma((nr,)), dma((nr,)), dma((nr,)), dma((nr,)), dma((2,)),
        ],
        compiler_params=pltpu.CompilerParams(collective_id=0, has_side_effects=True, vmem_limit_bytes=limit),
        name="fit_gather",
    )(amplitudes, aux_left, aux_right)

    rows = vc * og
    pad, wide_pad = up(rows, 8), up(rows, 16)
    cols = og * vir
    cols_pad = up(cols, 128)
    tiles = up(cols_pad, WIDE) // WIDE
    r, c = lax.axis_index("row"), lax.axis_index("col")
    vir_here = lax.dynamic_slice_in_dim(vir_energy, c * vc, vc)
    occ_here = lax.dynamic_slice_in_dim(occ_energy, r * og, og)
    rowd = (vir_here[None, :, None] - occ_energy.reshape(nr, 1, og)).reshape(nr, rows)
    rowd = jnp.pad(rowd, ((0, 0), (0, wide_pad - rows)), constant_values=1.0).reshape(nr * wide_pad, 1)
    rowd = jnp.broadcast_to(rowd, (nr * wide_pad, 128))
    cold = (vir_energy[None, :] - occ_here[:, None]).reshape(1, cols)
    cold = jnp.pad(cold, ((0, 0), (0, cols_pad - cols)), constant_values=1.0)
    cold = jnp.broadcast_to(cold, (8, cols_pad))

    moved = pl.pallas_call(
        functools.partial(tile_kernel, nr, og, vc, tiles),
        out_shape=jax.ShapeDtypeStruct((nr, pad, cols_pad), F32),
        in_specs=[vmem] * 6,
        out_specs=hbm,
        scratch_shapes=[
            pltpu.VMEM((vir, vir), BF16),
            pltpu.VMEM((vir, vir), BF16),
            pltpu.VMEM((cols_pad, naux), BF16),
            pltpu.VMEM((cols_pad, naux), BF16),
            pltpu.VMEM((half // 128, 2 * pad, 128), F32),
            pltpu.VMEM((2, 2 * pad, half), F32),
            pltpu.VMEM((nr, 2, 2 * pad, half), F32),
            pltpu.VMEM((2, nr * wide_pad, naux), BF16),
            pltpu.VMEM((2, nr * wide_pad, naux), BF16),
            pltpu.VMEM((2, nr * wide_pad, WIDE), F32),
            pltpu.VMEM((tiles, nr * wide_pad, WIDE), F32),
            pltpu.VMEM((nr * wide_pad, cols_pad), F32),
            dma((2, nr)), dma((2, nr)), dma((2,)), dma((tiles,)),
            dma((tiles, nr)), dma((tiles, nr)), dma((tiles,)),
        ],
        compiler_params=pltpu.CompilerParams(collective_id=1, has_side_effects=True, vmem_limit_bytes=limit),
        name="tile_exchange",
    )(fg, zg, left_rotation, right_rotation, rowd, cold)

    out = pl.pallas_call(
        functools.partial(lay_kernel, nr, og, vir, occ),
        grid=(pad // 8,),
        out_shape=jax.ShapeDtypeStruct((rows * occ, vir), F32),
        in_specs=[pl.BlockSpec((nr, 8, cols_pad), lambda g: (0, g, 0))],
        out_specs=pl.BlockSpec((8 * occ, vir), lambda g: (g, 0)),
        scratch_shapes=[pltpu.VMEM((up(vir, 128) // 128, 8 * occ, 128), F32)],
        compiler_params=pltpu.CompilerParams(vmem_limit_bytes=limit),
        name="lay_out",
    )(moved)
    return out.reshape(vc, og, occ, vir)


def solution(mesh):
    placed = (P("row", "col"), P("col", None), P("col", None), P(), P(), P(), P())
    return jax.shard_map(
        shards, mesh=mesh, in_specs=placed, out_specs=P("col", "row", None, None), check_vma=False
    )
```

time: 809 us -> 515 us (0.64); the launches traced: 796 us -> 515 us
  Pallas kernels: 0 us -> 506 us
  waiting for transfers between devices: 324 us -> 0 us
  local copies, waits for them, and re-layouts: 159 us -> 9.09 us
  matrix products: 128 us -> 0 us
  blocking collectives: 126 us -> 0 us
  starting transfers between devices: 23.4 us -> 0 us
  other arithmetic: 21 us -> 0.08 us
  between operations: 13.6 us -> 0.08 us
    pallas_call x0 -> x3, Pallas kernels: none -> 506 us  [the longest x1 263 us: shards(): pl.pallas_call(functools.partial(gather_kernel, nr, occ), out_shape=[jax....]
    all_to_all x4 -> x0, waiting for transfers between devices: 171 us -> none  [cut_exchange(): lax.all_to_all(section, axis, split_axis=0, concat_axis=0, tiled=True)]
    dot_general x4 -> x0, matrix products: 128 us -> none  [the longest x1 55 us: shards(): jnp.einsum('aibj,Bb->aijB', half_rot.reshape(vir_cols, occ_group, vir_cou...]
    all_to_all x1 -> x0, blocking collectives: 126 us -> none  [in_one_piece(): lax.all_to_all(both, axis, split_axis=split_dim, concat_axis=concat_dim,...]
    reduce_scatter x3 -> x0, waiting for transfers between devices: 96.9 us -> none  [own_block(): parts = lax.psum_scatter(parts, axes[k], scatter_dimension=0, tiled=True)]
    all_gather x1 -> x0, waiting for transfers between devices: 56.1 us -> none  [shards(): lax.all_gather(shared, COL, axis=0, tiled=True)]
    reshape x4 -> x0, local copies, waits for them, and re-layouts: 52.5 us -> none  [the longest x2 31.2 us: shards(): paired.reshape(vir_rows, occ_count, vir_cols, occ_count)]
    another operation x4 -> x0, local copies, waits for them, and re-layouts: 47 us -> none  [the longest x2 25.5 us: shards(): mirror_four = mirror.reshape(vir_cols, occ_group, vir_count, occ_count)]
  transfers between devices with their start and end apart: 8 -> 0, of which waited for: 8 -> 0; matrix products, arithmetic and copies ran while one was open for 2% -> 0% of each run, Pallas kernels for 0% -> 0%
where the time goes in v1:
time: 515 us
  Pallas kernels  506 us (98%)
  local copies, waits for them, and re-layouts  9.09 us (2%)
    pallas_call x1, Pallas kernels, shards(): pl.pallas_call(functools.partial(gather_kernel, nr, occ), out_shape=[jax....  263 us
    pallas_call x1, Pallas kernels, shards(): pl.pallas_call(functools.partial(tile_kernel, nr, og, vc, tiles), out_sha...  232 us
    pallas_call x1, Pallas kernels, shards(): pl.pallas_call(functools.partial(lay_kernel, nr, og, vir, occ), grid=(pad...  10.5 us

profile of v1, /device:TPU:48, one launch (start us, length us, event | category | flops | bytes accessed | tf_op | source)
XLA Modules:
  0.0 514.8 jit_solution(14386574155301423328)
XLA Ops:
  0.0 6.8 %copy.9.t_ref = f32[1600,800]{1,0:T(8,128)} copy(f32[1600,800]{0,1:T(8,128)} %param.7) | data formatting | bytes 10240000 | tf_op args[0]
  6.8 0.0 copy-start.1
  6.8 0.0 copy-start
  6.8 263.0 %fit_gather.1 = (f32[8,200,640]{2,1,0:T(8,128)}, f32[8,200,640]{2,1,0:T(8,128)}) custom-call(f32[1600,800]{1,0:T(8,128)} %copy.9.t_ref, f32[800,1280]{1,0:T(8,128)} %b_ref.1, f32[800,1280]{1,0:T(8,128)} %z_ref.1), custom_call_target="tpu_custom_call" | custom-call | tf_op jit(solution)/shard_map/fit_gather/pallas_call | solution.py:447
  269.9 0.0 copy-done.1
  269.9 0.1 sub.48
  270.0 0.1 sub.50
  270.1 0.0 copy-done
  270.1 0.1 dynamic_slice.6
  270.1 0.1 sub.45
  270.2 0.1 sub.46
  270.3 0.1 broadcast_in_dim.8
  270.4 1.0 broadcast_in_dim.18.rowd_ref
  271.4 0.1 dynamic_slice.7
  271.4 0.1 broadcast_subtract_fusion
  271.5 0.1 sub.55
  271.6 0.6 broadcast_in_dim.20.cold_ref
  272.3 232.0 %tile_exchange.1.in_ref = f32[8,104,1664]{2,1,0:T(8,128)} custom-call(f32[8,200,640]{2,1,0:T(8,128)} %get-tuple-element.7.fg_ref, f32[8,200,640]{2,1,0:T(8,128)} %get-tuple-element.8.zg_ref, f32[320,320]{1,0:T(8,128)} %l_ref.1, f32[320,320]{1,0:T(8,128)} %r_ref.1, f32[896,128]{1,0:T(8,128)} %broadcast_in_dim.18.rowd_ref, f32[8,1664]{1,0:T(8,128)} %broadcast_in_dim.20.cold_ref), custom_call_target="tpu_custom_call" | custom-call | tf_op jit(solution)/shard_map/tile_exchange/pallas_call | solution.py:487
  504.2 10.5 %lay_out.1 = f32[4000,320]{1,0:T(8,128)} custom-call(f32[8,104,1664]{2,1,0:T(8,128)} %tile_exchange.1.in_ref), custom_call_target="tpu_custom_call" | custom-call | tf_op jit(solution)/shard_map/lay_out/pallas_call | solution.py:512
  (4 shorter events, 0.0 us)
Async XLA Ops:
  6.8 263.0 %copy-start.1 = (f32[40]{0:T(128)S(1)}, f32[40]{0:T(128)}, u32[]{:S(2)}) copy-start(f32[40]{0:T(128)} %param.12) | copy-start | bytes 484
  6.8 263.2 %copy-start = (f32[320]{0:T(512)S(1)}, f32[320]{0:T(512)}, u32[]{:S(2)}) copy-start(f32[320]{0:T(512)} %param.13) | copy-start | bytes 3844

commit v2 on v1

--- a/solution.py
+++ b/solution.py
@@ -50,9 +50,9 @@
 def gather_kernel(
     nr, occ,
     t_ref, b_ref, z_ref,
-    fg_ref, zg_ref,
-    tp, zp, bh, bl, sib_send, sib_recv, own, rs_recv, fp, zs_send, zs_recv, zc,
-    sib_s, sib_r, rs_s, rs_r, zs_s, zs_r, za_s, za_r, fa_s, fa_r, loc,
+    fp_ref, zg_ref,
+    tp, zp, bh, bl, sib_send, sib_recv, own, rs_recv, zs_send, zs_recv, zc,
+    sib_s, sib_r, rs_s, rs_r, zs_s, zs_r, za_s, za_r, loc,
 ):
     r, c = lax.axis_index("row"), lax.axis_index("col")
     t, k = c // 2, lax.rem(c, 2)
@@ -133,7 +133,7 @@
         return 0
 
     lax.fori_loop(0, nr - 1, z_start, 0)
-    z_own = pltpu.make_async_copy(zc, zg_ref.at[t], loc.at[0])
+    z_own = pltpu.make_async_copy(zc, zg_ref.at[t], loc)
     z_own.start()
 
     def to_sibling(s):
@@ -143,18 +143,18 @@
         )
 
     def to_owner(s):
-        dst = lax.rem(r + 1 + s, nr)
+        dst = lax.rem(r + t + 1 + s, nr)
         return pltpu.make_async_remote_copy(
             src_ref=own.at[s], dst_ref=rs_recv.at[t], send_sem=rs_s.at[s], recv_sem=rs_r.at[t],
             device_id=(dst, 2 * lax.rem(r + dst, nr) + k), device_id_type=MESH,
         )
 
-    last_is_own = is_own
+    own_step = nr - 1 - t
 
     def finish(s):
         to_sibling(s).wait_recv()
         own[s] = own[s] + sib_recv[s]
-        here = jnp.logical_and(s == nr - 1, last_is_own)
+        here = jnp.logical_and(s == own_step, is_own)
 
         @pl.when(here)
         def _():
@@ -165,7 +165,7 @@
             to_owner(s).start()
 
     def step(s, _):
-        dst = lax.rem(r + 1 + s, nr)
+        dst = lax.rem(r + t + 1 + s, nr)
         x = jnp.concatenate(
             [every(tp, dst * og + ii, va, occ, t_ref.shape[1]) for ii in range(og)], axis=0
         )
@@ -201,23 +201,14 @@
         total = rs_recv[0, rows, :]
         for s in range(1, nr):
             total = total + rs_recv[s, rows, :]
-        fp[rows, :] = total
-        return 0
-
-    lax.fori_loop(0, fp.shape[0] // 8, add_up, 0)
-
-    def f_start(s, _):
-        spread(fp, fg_ref, blk, fa_s, fa_r, s).start()
-        return 0
-
-    lax.fori_loop(0, nr - 1, f_start, 0)
-    f_own = pltpu.make_async_copy(fp, fg_ref.at[blk], loc.at[1])
-    f_own.start()
+        fp_ref[rows, :] = total
+        return 0
+
+    lax.fori_loop(0, fp_ref.shape[0] // 8, add_up, 0)
 
     def settle(s, _):
         peer = lax.rem(t + 1 + s, nr)
         spread(zc, zg_ref, peer, za_s, za_r, s).wait()
-        spread(fp, fg_ref, lax.rem(peer - r + nr, nr), fa_s, fa_r, s).wait()
         return 0
 
     lax.fori_loop(0, nr - 1, settle, 0)
@@ -225,7 +216,7 @@
     def sent(s, _):
         to_sibling(s).wait_send()
 
-        @pl.when(jnp.logical_not(jnp.logical_and(s == nr - 1, last_is_own)))
+        @pl.when(jnp.logical_not(jnp.logical_and(s == own_step, is_own)))
         def _():
             to_owner(s).wait_send()
 
@@ -233,96 +224,164 @@
 
     lax.fori_loop(0, nr, sent, 0)
     z_own.wait()
-    f_own.wait()
 
 
 def tile_kernel(
-    nr, og, vc, tiles,
-    fg_ref, zg_ref, l_ref, r_ref, rowd_ref, cold_ref,
+    nr, og, vc, tiles, cuts,
+    fp_ref, zg_ref, l_ref, r_ref, rowd_ref, cold_ref,
     out_ref,
-    rh, rl, yh, yl, xp, xo, xg, xh, xl, s_send, s_recv, own,
-    xs, xr, ss, sr, os_, or_, loc,
+    fg, rh, rl, yh, yl, xp, xo, xg, xh, xl, s_send, s_recv, own,
+    fs, fr, xs, xr, ss, sr, os_, or_, loc,
 ):
     r, c = lax.axis_index("row"), lax.axis_index("col")
     t, k = c // 2, lax.rem(c, 2)
     sib = c + 1 - 2 * k
-    half = fg_ref.shape[2]
+    half = fp_ref.shape[1]
     vir = r_ref.shape[0]
     va = vir // nr
     pad = xo.shape[1] // 2
     wide_pad = xh.shape[1] // nr
+    blk = lax.rem(t - r + nr, nr)
+    far = r + 1 - 2 * lax.rem(r, 2)
+    near = nr // 2 - 1
 
     barrier = pltpu.get_barrier_semaphore()
     pl.semaphore_signal(barrier, inc=1, device_id=(r, sib), device_id_type=MESH)
 
     def greet(s, _):
         pl.semaphore_signal(barrier, inc=1, device_id=(lax.rem(r + 1 + s, nr), c), device_id_type=MESH)
+        pl.semaphore_signal(
+            barrier, inc=1, device_id=(r, 2 * lax.rem(t + 1 + s, nr) + k), device_id_type=MESH
+        )
         return 0
 
     lax.fori_loop(0, nr - 1, greet, 0)
 
     hi, lo = halves(r_ref[...])
-    rh[...] = hi
-    rl[...] = lo
-    lh, ll = halves(l_ref[pl.ds(pl.multiple_of(t * va, 8), va), :])
+    rh[:vir, :] = hi
+    rl[:vir, :] = lo
+    hi, lo = halves(l_ref[pl.ds(pl.multiple_of(t * va, 8), va), :])
+    rh[vir:, :] = hi
+    rl[vir:, :] = lo
     xp[...] = jnp.zeros_like(xp)
-    pl.semaphore_wait(barrier, nr)
-
-    def x_copy(q, s):
-        return pltpu.make_async_remote_copy(
-            src_ref=xo.at[q], dst_ref=xg.at[r, q], send_sem=xs.at[q, s], recv_sem=xr.at[q, r],
-            device_id=(lax.rem(r + 1 + s, nr), c), device_id_type=MESH,
-        )
-
-    def x_wait(q, s):
-        src = lax.rem(r + 1 + s, nr)
-        return pltpu.make_async_remote_copy(
-            src_ref=xo.at[q], dst_ref=xg.at[src, q], send_sem=xs.at[q, s], recv_sem=xr.at[q, src],
-            device_id=(src, c), device_id_type=MESH,
-        )
-
-    for q, g_ref in ((1, zg_ref), (0, fg_ref)):
-        y_at = (1 - q) * half
+    fg[blk] = fp_ref[...]
+    pl.semaphore_wait(barrier, 2 * nr - 1)
+
+    def f_copy(m, s):
+        at, width = cuts[m]
+        cols = pl.ds(at, width)
+        return pltpu.make_async_remote_copy(
+            src_ref=fp_ref.at[:, cols], dst_ref=fg.at[blk, :, cols],
+            send_sem=fs.at[m, s], recv_sem=fr.at[m, blk],
+            device_id=(r, 2 * lax.rem(t + 1 + s, nr) + k), device_id_type=MESH,
+        )
+
+    def f_wait(m, s):
+        at, width = cuts[m]
+        cols = pl.ds(at, width)
+        peer = lax.rem(t + 1 + s, nr)
+        slot = lax.rem(peer - r + nr, nr)
+        return pltpu.make_async_remote_copy(
+            src_ref=fp_ref.at[:, cols], dst_ref=fg.at[slot, :, cols],
+            send_sem=fs.at[m, s], recv_sem=fr.at[m, slot],
+            device_id=(r, 2 * peer + k), device_id_type=MESH,
+        )
+
+    def each(count, body):
+        def one(s, _):
+            body(s)
+            return 0
+
+        lax.fori_loop(0, count, one, 0)
+
+    for m in range(len(cuts)):
+        each(nr - 1, lambda s, m=m: f_copy(m, s).start())
+
+    def x_cut(m):
+        return (1, 0, half) if m == len(cuts) else (0,) + cuts[m]
+
+    def x_push(m, src_ref, slot, dst, sem):
+        return pltpu.make_async_remote_copy(
+            src_ref=src_ref, dst_ref=xg.at[slot, x_cut(m)[0], :, pl.ds(*x_cut(m)[1:])],
+            send_sem=xs.at[m, sem], recv_sem=xr.at[m, slot],
+            device_id=(dst, c), device_id_type=MESH,
+        )
+
+    def x_mine(m):
+        q, at, width = x_cut(m)
+        return xo.at[q, :, pl.ds(at, width)]
+
+    def x_far(m):
+        q, at, width = x_cut(m)
+        return xg.at[far, q, :, pl.ds(at, width)]
+
+    def beside(s):
+        return lax.rem(r + 2 * (s + 1), nr)
+
+    def x_start(m):
+        x_push(m, x_mine(m), r, far, near).start()
+        each(near, lambda s: x_push(m, x_mine(m), r, beside(s), s).start())
+
+    def x_arrive(m, slot):
+        x_push(m, x_mine(m), slot, far, near).wait_recv()
+
+    def x_forward(m):
+        x_arrive(m, far)
+        each(near, lambda s: x_push(m, x_far(m), far, beside(s), near + 1 + s).start())
+
+    def rotate(g_ref, q, at, width):
+        y_at = (1 - q) * half + at
         for ii in range(og):
-            gh, gl = halves(g_ref[:, ii * va : (ii + 1) * va, :].reshape(vir, half))
-            x = dot3(lh, ll, gh, gl, ((1,), (0,)))
+            gh, gl = halves(g_ref[:, ii * va : (ii + 1) * va, at : at + width].reshape(vir, width))
+            both = dot3(rh[...], rl[...], gh, gl, ((1,), (0,)))
+            hi, lo = halves(both[:vir])
+            yh[ii * vir : (ii + 1) * vir, y_at : y_at + width] = hi
+            yl[ii * vir : (ii + 1) * vir, y_at : y_at + width] = lo
             for par in range(2):
-                for p in range(half // 128):
-                    xp[p, pl.ds(par * pad + ii, vc, stride=og), :] = x[
-                        par * vc : (par + 1) * vc, p * 128 : (p + 1) * 128
-                    ]
-            y = dot3(rh[...], rl[...], gh, gl, ((1,), (0,)))
-            hi, lo = halves(y)
-            yh[ii * vir : (ii + 1) * vir, y_at : y_at + half] = hi
-            yl[ii * vir : (ii + 1) * vir, y_at : y_at + half] = lo
-
-        for p in range(half // 128):
-            xo[q, :, p * 128 : (p + 1) * 128] = xp[p]
-
-        def x_start(s, _, q=q):
-            x_copy(q, s).start()
-            return 0
-
-        lax.fori_loop(0, nr - 1, x_start, 0)
-
-    def take(src, q, load):
-        x_at = q * half
-        at = pl.multiple_of(src * wide_pad, 16)
+                rows = both[vir + par * vc : vir + (par + 1) * vc]
+                for p in range(width // 128):
+                    xp[p, pl.ds(par * pad + ii, vc, stride=og), :] = rows[:, p * 128 : (p + 1) * 128]
+        for p in range(width // 128):
+            xo[q, :, at + p * 128 : at + (p + 1) * 128] = xp[p]
+
+    def take(m, src, load):
+        q, at, width = x_cut(m)
+        x_at = q * half + at
+        rows = pl.ds(pl.multiple_of(src * wide_pad, 16), pad)
         for par in range(2):
-            hi, lo = halves(load(par))
-            xh[par, pl.ds(at, pad), x_at : x_at + half] = hi
-            xl[par, pl.ds(at, pad), x_at : x_at + half] = lo
-
-    for q in (1, 0):
-        take(r, q, lambda par, q=q: xo[q, par * pad : (par + 1) * pad, :])
-
-        def x_take(s, _, q=q):
-            src = lax.rem(r + 1 + s, nr)
-            x_wait(q, s).wait_recv()
-            take(src, q, lambda par: xg[src, q, par * pad : (par + 1) * pad, :])
-            return 0
-
-        lax.fori_loop(0, nr - 1, x_take, 0)
+            hi, lo = halves(load(q, par * pad, at, width))
+            xh[par, rows, x_at : x_at + width] = hi
+            xl[par, rows, x_at : x_at + width] = lo
+
+    def take_own(m):
+        take(m, r, lambda q, row, at, width: xo[q, row : row + pad, at : at + width])
+
+    def take_from(m, src):
+        take(m, src, lambda q, row, at, width: xg[src, q, row : row + pad, at : at + width])
+
+    def take_near(m, base):
+        def one(s):
+            src = lax.rem(base + 2 * (s + 1), nr)
+            x_arrive(m, src)
+            take_from(m, src)
+
+        each(near, one)
+
+    zm = len(cuts)
+    rotate(zg_ref, 1, 0, half)
+    x_start(zm)
+    order = [zm] + list(range(zm))
+    for m, (at, width) in enumerate(cuts):
+        each(nr - 1, lambda s, m=m: f_wait(m, s).wait_recv())
+        rotate(fg, 0, at, width)
+        x_start(m)
+        x_forward(order[m])
+    x_forward(order[-1])
+    for m in order:
+        take_own(m)
+        take_from(m, far)
+        take_near(m, r)
+        take_near(m, far)
 
     def to_sibling(n, width):
         return pltpu.make_async_remote_copy(
@@ -365,15 +424,15 @@
         reps = width // 128
 
         def close(g, _):
-            at = pl.ds(pl.multiple_of(g * 8, 8), 8)
+            at = pl.ds(pl.multiple_of(g * wide_pad, 8), wide_pad)
             rowd = rowd_ref[at, :]
             for m in range(reps):
                 cols = pl.ds(pl.multiple_of(n * WIDE + m * 128, 128), 128)
                 here = own[at, cols] + s_recv[n, at, m * 128 : (m + 1) * 128]
-                own[at, cols] = here / (rowd + cold_ref[:, cols])
+                own[at, cols] = here / (rowd + cold_ref[0:1, cols])
             return 0
 
-        lax.fori_loop(0, own.shape[0] // 8, close, 0)
+        lax.fori_loop(0, nr, close, 0)
 
         def send(s, _):
             to_row(n, width, s, r).start()
@@ -408,12 +467,12 @@
     settle(jnp.int32(tiles - 1), tail)
     to_sibling(jnp.int32(tiles - 2), WIDE).wait_send()
     to_sibling(jnp.int32(tiles - 1), tail).wait_send()
-    for q in (1, 0):
-        def x_sent(s, _, q=q):
-            x_copy(q, s).wait_send()
-            return 0
-
-        lax.fori_loop(0, nr - 1, x_sent, 0)
+    for m in order:
+        x_push(m, x_mine(m), r, far, near).wait_send()
+        each(near, lambda s, m=m: x_push(m, x_mine(m), r, beside(s), s).wait_send())
+        each(near, lambda s, m=m: x_push(m, x_far(m), far, beside(s), near + 1 + s).wait_send())
+    for m in range(zm):
+        each(nr - 1, lambda s, m=m: f_copy(m, s).wait_send())
 
 
 def lay_kernel(nr, og, vir, occ, in_ref, out_ref, op):
@@ -444,11 +503,14 @@
     hbm = pl.BlockSpec(memory_space=pl.ANY)
     limit = 60 * 1024 * 1024
 
-    fg, zg = pl.pallas_call(
+    fp, zg = pl.pallas_call(
         functools.partial(gather_kernel, nr, occ),
-        out_shape=[jax.ShapeDtypeStruct((nr, piece, half), F32)] * 2,
+        out_shape=[
+            jax.ShapeDtypeStruct((piece, half), F32),
+            jax.ShapeDtypeStruct((nr, piece, half), F32),
+        ],
         in_specs=[vmem] * 3,
-        out_specs=[hbm] * 2,
+        out_specs=[vmem, hbm],
         scratch_shapes=[
             pltpu.VMEM((up(amplitudes.shape[1], 128) // 128, amplitudes.shape[0], 128), F32),
             pltpu.VMEM((up(naux, 128) // 128, aux_right.shape[0], 128), F32),
@@ -458,12 +520,11 @@
             pltpu.VMEM((nr, piece, half), F32),
             pltpu.VMEM((nr, piece, half), F32),
             pltpu.VMEM((nr, piece, half), F32),
-            pltpu.VMEM((piece, half), F32),
             pltpu.VMEM((og, vc, half), F32),
             pltpu.VMEM((og, vc, half), F32),
             pltpu.VMEM((piece, half), F32),
             dma((nr,)), dma((nr,)), dma((nr,)), dma((nr,)), dma, dma,
-            dma((nr,)), dma((nr,)), dma((nr,)), dma((nr,)), dma((2,)),
+            dma((nr,)), dma((nr,)), dma,
         ],
         compiler_params=pltpu.CompilerParams(collective_id=0, has_side_effects=True, vmem_limit_bytes=limit),
         name="fit_gather",
@@ -474,6 +535,7 @@
     cols = og * vir
     cols_pad = up(cols, 128)
     tiles = up(cols_pad, WIDE) // WIDE
+    cuts = [(at, min(256, half - at)) for at in range(0, half, 256)]
     r, c = lax.axis_index("row"), lax.axis_index("col")
     vir_here = lax.dynamic_slice_in_dim(vir_energy, c * vc, vc)
     occ_here = lax.dynamic_slice_in_dim(occ_energy, r * og, og)
@@ -485,13 +547,14 @@
     cold = jnp.broadcast_to(cold, (8, cols_pad))
 
     moved = pl.pallas_call(
-        functools.partial(tile_kernel, nr, og, vc, tiles),
+        functools.partial(tile_kernel, nr, og, vc, tiles, cuts),
         out_shape=jax.ShapeDtypeStruct((nr, pad, cols_pad), F32),
         in_specs=[vmem] * 6,
         out_specs=hbm,
         scratch_shapes=[
-            pltpu.VMEM((vir, vir), BF16),
-            pltpu.VMEM((vir, vir), BF16),
+            pltpu.VMEM((nr, piece, half), F32),
+            pltpu.VMEM((vir + va, vir), BF16),
+            pltpu.VMEM((vir + va, vir), BF16),
             pltpu.VMEM((cols_pad, naux), BF16),
             pltpu.VMEM((cols_pad, naux), BF16),
             pltpu.VMEM((half // 128, 2 * pad, 128), F32),
@@ -502,12 +565,13 @@
             pltpu.VMEM((2, nr * wide_pad, WIDE), F32),
             pltpu.VMEM((tiles, nr * wide_pad, WIDE), F32),
             pltpu.VMEM((nr * wide_pad, cols_pad), F32),
-            dma((2, nr)), dma((2, nr)), dma((2,)), dma((tiles,)),
+            dma((len(cuts), nr)), dma((len(cuts), nr)),
+            dma((len(cuts) + 1, nr)), dma((len(cuts) + 1, nr)), dma((2,)), dma((tiles,)),
             dma((tiles, nr)), dma((tiles, nr)), dma((tiles,)),
         ],
         compiler_params=pltpu.CompilerParams(collective_id=1, has_side_effects=True, vmem_limit_bytes=limit),
         name="tile_exchange",
-    )(fg, zg, left_rotation, right_rotation, rowd, cold)
+    )(fp, zg, left_rotation, right_rotation, rowd, cold)
 
     out = pl.pallas_call(
         functools.partial(lay_kernel, nr, og, vir, occ),

time: 515 us -> 435 us (0.84)
  Pallas kernels: 506 us -> 419 us
    pallas_call x1, Pallas kernels: 263 us -> 198 us  [shards(): pl.pallas_call(functools.partial(gather_kernel, nr, occ), out_shape=[jax....]
    pallas_call x1, Pallas kernels: 232 us -> 210 us  [shards(): pl.pallas_call(functools.partial(tile_kernel, nr, og, vc, tiles, cuts), o...]
where the time goes in v2:
time: 435 us; the launch traced here: 431 us
  Pallas kernels  419 us (96%)
  local copies, waits for them, and re-layouts  11.1 us (3%)
    pallas_call x1, Pallas kernels, shards(): pl.pallas_call(functools.partial(tile_kernel, nr, og, vc, tiles, cuts), o...  210 us
    pallas_call x1, Pallas kernels, shards(): pl.pallas_call(functools.partial(gather_kernel, nr, occ), out_shape=[jax....  198 us
    pallas_call x1, Pallas kernels, shards(): pl.pallas_call(functools.partial(lay_kernel, nr, og, vir, occ), grid=(pad...  10.5 us

profile of v2, /device:TPU:48, one launch (start us, length us, event | category | flops | bytes accessed | tf_op | source)
XLA Modules:
  0.0 430.7 jit_solution(16108042767046983650)
XLA Ops:
  0.0 0.7 dynamic_slice.7
  0.7 0.8 dynamic_slice.6
  1.5 0.7 sub.48
  2.2 0.1 sub.45
  2.3 0.1 sub.46
  2.4 0.8 broadcast_subtract_fusion
  3.1 0.1 sub.55
  3.2 0.6 broadcast_in_dim.20.cold_ref
  3.9 0.1 sub.50
  4.0 0.1 broadcast_in_dim.8
  4.1 0.9 broadcast_in_dim.18.rowd_ref
  5.0 6.8 %copy.9.t_ref = f32[1600,800]{1,0:T(8,128)} copy(f32[1600,800]{0,1:T(8,128)} %param.7) | data formatting | bytes 10240000 | tf_op args[0]
  11.8 197.8 %fit_gather.1 = (f32[200,640]{1,0:T(8,128)}, f32[8,200,640]{2,1,0:T(8,128)}) custom-call(f32[1600,800]{1,0:T(8,128)} %copy.9.t_ref, f32[800,1280]{1,0:T(8,128)} %b_ref.1, f32[800,1280]{1,0:T(8,128)} %z_ref.1), custom_call_target="tpu_custom_call" | custom-call | tf_op jit(solution)/shard_map/fit_gather/pallas_call | solution.py:506
  209.7 210.5 %tile_exchange.1.in_ref = f32[8,104,1664]{2,1,0:T(8,128)} custom-call(f32[200,640]{1,0:T(8,128)} %get-tuple-element.7.fp_ref, f32[8,200,640]{2,1,0:T(8,128)} %get-tuple-element.8.zg_ref, f32[320,320]{1,0:T(8,128)} %l_ref.1, f32[320,320]{1,0:T(8,128)} %r_ref.1, f32[896,128]{1,0:T(8,128)} %broadcast_in_dim.18.rowd_ref, f32[8,1664]{1,0:T(8,128)} %broadcast_in_dim.20.cold_ref), custom_call_target="tpu_custom_call" | custom-call | tf_op jit(solution)/shard_map/tile_exchange/pallas_call | solution.py:549
  420.2 10.5 %lay_out.1 = f32[4000,320]{1,0:T(8,128)} custom-call(f32[8,104,1664]{2,1,0:T(8,128)} %tile_exchange.1.in_ref), custom_call_target="tpu_custom_call" | custom-call | tf_op jit(solution)/shard_map/lay_out/pallas_call | solution.py:576
  (4 shorter events, 0.0 us)

commit v3 on v2

--- a/solution.py
+++ b/solution.py
@@ -51,8 +51,8 @@
     nr, occ,
     t_ref, b_ref, z_ref,
     fp_ref, zg_ref,
-    tp, zp, bh, bl, sib_send, sib_recv, own, rs_recv, zs_send, zs_recv, zc,
-    sib_s, sib_r, rs_s, rs_r, zs_s, zs_r, za_s, za_r, loc,
+    tp, zp, bh, bl, sib_send, sib_recv, own, z_recv, rs_recv, zs_send, zs_recv, zc,
+    sib_s, sib_r, zz_s, zz_r, rs_s, rs_r, zs_s, zs_r, za_s, za_r, loc,
 ):
     r, c = lax.axis_index("row"), lax.axis_index("col")
     t, k = c // 2, lax.rem(c, 2)
@@ -63,25 +63,40 @@
     half = b_ref.shape[1] // 2
     blk = lax.rem(t - r + nr, nr)
     is_own = lax.rem(r + r, nr) == t
+    ny = nr // 2
+    y, low = t // 2, lax.rem(t, 2)
+    pair = t + 1 - 2 * low
 
     barrier = pltpu.get_barrier_semaphore()
     pl.semaphore_signal(barrier, inc=1, device_id=(r, sib), device_id_type=MESH)
 
-    def greet(s, _):
-        peer = lax.rem(t + 1 + s, nr)
-        pl.semaphore_signal(barrier, inc=1, device_id=(r, 2 * peer + k), device_id_type=MESH)
-        return 0
-
-    lax.fori_loop(0, nr - 1, greet, 0)
-
-    def greet_sources(s, _):
-        @pl.when(jnp.logical_not(jnp.logical_and(is_own, s == t)))
-        def _():
-            pl.semaphore_signal(barrier, inc=1, device_id=(blk, 2 * s + k), device_id_type=MESH)
-
-        return 0
-
-    lax.fori_loop(0, nr, greet_sources, 0)
+    pl.semaphore_signal(barrier, inc=1, device_id=(r, 2 * pair + k), device_id_type=MESH)
+
+    def along(s):
+        return 2 * lax.rem(y + 1 + s, ny) + low
+
+    def each(count, body):
+        def one(s, _):
+            body(s)
+            return 0
+
+        lax.fori_loop(0, count, one, 0)
+
+    each(
+        ny - 1,
+        lambda s: pl.semaphore_signal(
+            barrier, inc=1, device_id=(r, 2 * along(s) + k), device_id_type=MESH
+        ),
+    )
+
+    def greet_source(s):
+        @pl.when(jnp.logical_not(jnp.logical_and(is_own, s == y)))
+        def _():
+            pl.semaphore_signal(
+                barrier, inc=1, device_id=(blk, 2 * (2 * s + low) + k), device_id_type=MESH
+            )
+
+    each(ny, greet_source)
 
     planes(t_ref, tp)
     planes(z_ref, zp)
@@ -102,11 +117,11 @@
 
     @pl.when(is_own)
     def _():
-        pl.semaphore_wait(barrier, 2 * nr - 1)
+        pl.semaphore_wait(barrier, nr)
 
     @pl.when(jnp.logical_not(is_own))
     def _():
-        pl.semaphore_wait(barrier, 2 * nr)
+        pl.semaphore_wait(barrier, nr + 1)
 
     z_swap = pltpu.make_async_remote_copy(
         src_ref=zs_send, dst_ref=zs_recv, send_sem=zs_s, recv_sem=zs_r,
@@ -121,18 +136,14 @@
             [jnp.where(first, z_mine, z_sib), jnp.where(first, z_sib, z_mine)], axis=0
         )
 
-    def spread(src, dst, slot, send, recv, s):
-        peer = lax.rem(t + 1 + s, nr)
-        return pltpu.make_async_remote_copy(
-            src_ref=src, dst_ref=dst.at[slot], send_sem=send.at[s], recv_sem=recv.at[slot],
+    def z_push(src_ref, slot, peer, sem):
+        return pltpu.make_async_remote_copy(
+            src_ref=src_ref, dst_ref=zg_ref.at[slot], send_sem=za_s.at[sem], recv_sem=za_r.at[slot],
             device_id=(r, 2 * peer + k), device_id_type=MESH,
         )
 
-    def z_start(s, _):
-        spread(zc, zg_ref, t, za_s, za_r, s).start()
-        return 0
-
-    lax.fori_loop(0, nr - 1, z_start, 0)
+    z_push(zc, t, pair, ny - 1).start()
+    each(ny - 1, lambda s: z_push(zc, t, along(s), s).start())
     z_own = pltpu.make_async_copy(zc, zg_ref.at[t], loc)
     z_own.start()
 
@@ -142,30 +153,34 @@
             device_id=(r, sib), device_id_type=MESH,
         )
 
+    def owner(s):
+        stays = s // ny
+        side = stays * low + (1 - stays) * (1 - low)
+        return 2 * lax.rem(y + 1 + lax.rem(s, ny), ny) + side
+
+    def to_pair(s):
+        return pltpu.make_async_remote_copy(
+            src_ref=own.at[s], dst_ref=z_recv.at[s], send_sem=zz_s.at[s], recv_sem=zz_r.at[s],
+            device_id=(r, 2 * pair + k), device_id_type=MESH,
+        )
+
     def to_owner(s):
-        dst = lax.rem(r + t + 1 + s, nr)
-        return pltpu.make_async_remote_copy(
-            src_ref=own.at[s], dst_ref=rs_recv.at[t], send_sem=rs_s.at[s], recv_sem=rs_r.at[t],
-            device_id=(dst, 2 * lax.rem(r + dst, nr) + k), device_id_type=MESH,
-        )
-
-    own_step = nr - 1 - t
+        ot = owner(ny + s)
+        return pltpu.make_async_remote_copy(
+            src_ref=own.at[ny + s], dst_ref=rs_recv.at[y], send_sem=rs_s.at[s], recv_sem=rs_r.at[y],
+            device_id=(lax.rem(ot - r + nr, nr), 2 * ot + k), device_id_type=MESH,
+        )
 
     def finish(s):
         to_sibling(s).wait_recv()
         own[s] = own[s] + sib_recv[s]
-        here = jnp.logical_and(s == own_step, is_own)
-
-        @pl.when(here)
-        def _():
-            rs_recv[t] = own[s]
-
-        @pl.when(jnp.logical_not(here))
-        def _():
-            to_owner(s).start()
-
-    def step(s, _):
-        dst = lax.rem(r + t + 1 + s, nr)
+
+        @pl.when(s < ny)
+        def _():
+            to_pair(s).start()
+
+    def step(s):
+        dst = lax.rem(owner(s) - r + nr, nr)
         x = jnp.concatenate(
             [every(tp, dst * og + ii, va, occ, t_ref.shape[1]) for ii in range(og)], axis=0
         )
@@ -179,50 +194,66 @@
         def _():
             finish(s - 1)
 
-        return 0
-
-    lax.fori_loop(0, nr, step, 0)
+    each(nr, step)
     finish(nr - 1)
 
-    def arrived(s, _):
-        @pl.when(jnp.logical_not(jnp.logical_and(is_own, s == t)))
+    z_push(zc, pair, pair, ny - 1).wait_recv()
+    each(ny - 1, lambda s: z_push(zg_ref.at[pair], pair, along(s), ny + s).start())
+
+    def deliver(s):
+        to_pair(s).wait_recv()
+        own[ny + s] = own[ny + s] + z_recv[s]
+        here = jnp.logical_and(s == ny - 1, is_own)
+
+        @pl.when(here)
+        def _():
+            rs_recv[y] = own[ny + s]
+
+        @pl.when(jnp.logical_not(here))
+        def _():
+            to_owner(s).start()
+
+    each(ny, deliver)
+
+    def arrived(s):
+        @pl.when(jnp.logical_not(jnp.logical_and(is_own, s == y)))
         def _():
             pltpu.make_async_remote_copy(
                 src_ref=own.at[0], dst_ref=rs_recv.at[s], send_sem=rs_s.at[0], recv_sem=rs_r.at[s],
                 device_id=(r, sib), device_id_type=MESH,
             ).wait_recv()
 
-        return 0
-
-    lax.fori_loop(0, nr, arrived, 0)
+    each(ny, arrived)
 
     def add_up(g, _):
         rows = pl.ds(pl.multiple_of(g * 8, 8), 8)
         total = rs_recv[0, rows, :]
-        for s in range(1, nr):
+        for s in range(1, ny):
             total = total + rs_recv[s, rows, :]
         fp_ref[rows, :] = total
         return 0
 
     lax.fori_loop(0, fp_ref.shape[0] // 8, add_up, 0)
 
-    def settle(s, _):
-        peer = lax.rem(t + 1 + s, nr)
-        spread(zc, zg_ref, peer, za_s, za_r, s).wait()
-        return 0
-
-    lax.fori_loop(0, nr - 1, settle, 0)
-
-    def sent(s, _):
-        to_sibling(s).wait_send()
-
-        @pl.when(jnp.logical_not(jnp.logical_and(s == own_step, is_own)))
+    z_push(zc, t, pair, ny - 1).wait_send()
+
+    def settle(s):
+        z_push(zc, t, along(s), s).wait_send()
+        z_push(zc, along(s), along(s), s).wait_recv()
+        z_push(zg_ref.at[pair], pair, along(s), ny + s).wait_send()
+        z_push(zc, along(s) + pair - t, pair, s).wait_recv()
+
+    each(ny - 1, settle)
+    each(nr, lambda s: to_sibling(s).wait_send())
+
+    def sent(s):
+        to_pair(s).wait_send()
+
+        @pl.when(jnp.logical_not(jnp.logical_and(s == ny - 1, is_own)))
         def _():
             to_owner(s).wait_send()
 
-        return 0
-
-    lax.fori_loop(0, nr, sent, 0)
+    each(ny, sent)
     z_own.wait()
 
 
@@ -267,23 +298,22 @@
     fg[blk] = fp_ref[...]
     pl.semaphore_wait(barrier, 2 * nr - 1)
 
-    def f_copy(m, s):
+    ny = nr // 2
+    y, low = t // 2, lax.rem(t, 2)
+    pair = t + 1 - 2 * low
+
+    def along(s):
+        return 2 * lax.rem(y + 1 + s, ny) + low
+
+    def slot_of(other):
+        return lax.rem(other - r + nr, nr)
+
+    def f_push(m, src_ref, slot, peer, sem):
         at, width = cuts[m]
         cols = pl.ds(at, width)
         return pltpu.make_async_remote_copy(
-            src_ref=fp_ref.at[:, cols], dst_ref=fg.at[blk, :, cols],
-            send_sem=fs.at[m, s], recv_sem=fr.at[m, blk],
-            device_id=(r, 2 * lax.rem(t + 1 + s, nr) + k), device_id_type=MESH,
-        )
-
-    def f_wait(m, s):
-        at, width = cuts[m]
-        cols = pl.ds(at, width)
-        peer = lax.rem(t + 1 + s, nr)
-        slot = lax.rem(peer - r + nr, nr)
-        return pltpu.make_async_remote_copy(
-            src_ref=fp_ref.at[:, cols], dst_ref=fg.at[slot, :, cols],
-            send_sem=fs.at[m, s], recv_sem=fr.at[m, slot],
+            src_ref=src_ref.at[:, cols], dst_ref=fg.at[slot, :, cols],
+            send_sem=fs.at[m, sem], recv_sem=fr.at[m, slot],
             device_id=(r, 2 * peer + k), device_id_type=MESH,
         )
 
@@ -294,8 +324,26 @@
 
         lax.fori_loop(0, count, one, 0)
 
+    def f_start(m):
+        f_push(m, fp_ref, blk, pair, ny - 1).start()
+        each(ny - 1, lambda s: f_push(m, fp_ref, blk, along(s), s).start())
+
+    def f_forward(m):
+        f_push(m, fp_ref, slot_of(pair), pair, ny - 1).wait_recv()
+        each(
+            ny - 1,
+            lambda s: f_push(m, fg.at[slot_of(pair)], slot_of(pair), along(s), ny + s).start(),
+        )
+
+    def f_rest(m):
+        def one(s):
+            f_push(m, fp_ref, slot_of(along(s)), pair, ny - 1).wait_recv()
+            f_push(m, fp_ref, slot_of(along(s) + pair - t), pair, ny - 1).wait_recv()
+
+        each(ny - 1, one)
+
     for m in range(len(cuts)):
-        each(nr - 1, lambda s, m=m: f_copy(m, s).start())
+        f_start(m)
 
     def x_cut(m):
         return (1, 0, half) if m == len(cuts) else (0,) + cuts[m]
@@ -370,9 +418,11 @@
     zm = len(cuts)
     rotate(zg_ref, 1, 0, half)
     x_start(zm)
+    for m in range(zm):
+        f_forward(m)
     order = [zm] + list(range(zm))
     for m, (at, width) in enumerate(cuts):
-        each(nr - 1, lambda s, m=m: f_wait(m, s).wait_recv())
+        f_rest(m)
         rotate(fg, 0, at, width)
         x_start(m)
         x_forward(order[m])
@@ -472,7 +522,9 @@
         each(near, lambda s, m=m: x_push(m, x_mine(m), r, beside(s), s).wait_send())
         each(near, lambda s, m=m: x_push(m, x_far(m), far, beside(s), near + 1 + s).wait_send())
     for m in range(zm):
-        each(nr - 1, lambda s, m=m: f_copy(m, s).wait_send())
+        f_push(m, fp_ref, blk, pair, ny - 1).wait_send()
+        each(ny - 1, lambda s, m=m: f_push(m, fp_ref, blk, along(s), s).wait_send())
+        each(ny - 1, lambda s, m=m: f_push(m, fp_ref, blk, along(s), ny + s).wait_send())
 
 
 def lay_kernel(nr, og, vir, occ, in_ref, out_ref, op):
@@ -519,11 +571,12 @@
             pltpu.VMEM((nr, piece, half), F32),
             pltpu.VMEM((nr, piece, half), F32),
             pltpu.VMEM((nr, piece, half), F32),
-            pltpu.VMEM((nr, piece, half), F32),
+            pltpu.VMEM((nr // 2, piece, half), F32),
+            pltpu.VMEM((nr // 2, piece, half), F32),
             pltpu.VMEM((og, vc, half), F32),
             pltpu.VMEM((og, vc, half), F32),
             pltpu.VMEM((piece, half), F32),
-            dma((nr,)), dma((nr,)), dma((nr,)), dma((nr,)), dma, dma,
+            dma((nr,)), dma((nr,)), dma((nr,)), dma((nr,)), dma((nr,)), dma((nr,)), dma, dma,
             dma((nr,)), dma((nr,)), dma,
         ],
         compiler_params=pltpu.CompilerParams(collective_id=0, has_side_effects=True, vmem_limit_bytes=limit),

time: 435 us -> 337 us (0.77)
  Pallas kernels: 419 us -> 320 us
    pallas_call x1, Pallas kernels: 198 us -> 113 us  [shards(): pl.pallas_call(functools.partial(gather_kernel, nr, occ), out_shape=[jax....]
    pallas_call x1, Pallas kernels: 210 us -> 196 us  [shards(): pl.pallas_call(functools.partial(tile_kernel, nr, og, vc, tiles, cuts), o...]
where the time goes in v3:
time: 337 us; the launch traced here: 332 us
  Pallas kernels  320 us (95%)
  local copies, waits for them, and re-layouts  11.1 us (3%)
    pallas_call x1, Pallas kernels, shards(): pl.pallas_call(functools.partial(tile_kernel, nr, og, vc, tiles, cuts), o...  196 us
    pallas_call x1, Pallas kernels, shards(): pl.pallas_call(functools.partial(gather_kernel, nr, occ), out_shape=[jax....  113 us
    pallas_call x1, Pallas kernels, shards(): pl.pallas_call(functools.partial(lay_kernel, nr, og, vir, occ), grid=(pad...  10.5 us
    unnamed x1, local copies, waits for them, and re-layouts  6.83 us

profile of v3, /device:TPU:48, one launch (start us, length us, event | category | flops | bytes accessed | tf_op | source)
XLA Modules:
  0.0 331.7 jit_solution(2373257118813160197)
XLA Ops:
  0.0 0.7 dynamic_slice.7
  0.7 0.8 dynamic_slice.6
  1.5 0.7 sub.48
  2.2 0.1 sub.45
  2.3 0.1 sub.46
  2.4 0.8 broadcast_subtract_fusion
  3.1 0.1 sub.55
  3.2 0.6 broadcast_in_dim.20.cold_ref
  3.9 0.1 sub.50
  4.0 0.1 broadcast_in_dim.8
  4.1 0.9 broadcast_in_dim.18.rowd_ref
  5.0 6.8 %copy.9.t_ref = f32[1600,800]{1,0:T(8,128)} copy(f32[1600,800]{0,1:T(8,128)} %param.7) | data formatting | bytes 10240000 | tf_op args[0]
  11.8 113.1 %fit_gather.1 = (f32[200,640]{1,0:T(8,128)}, f32[8,200,640]{2,1,0:T(8,128)}) custom-call(f32[1600,800]{1,0:T(8,128)} %copy.9.t_ref, f32[800,1280]{1,0:T(8,128)} %b_ref.1, f32[800,1280]{1,0:T(8,128)} %z_ref.1), custom_call_target="tpu_custom_call" | custom-call | tf_op jit(solution)/shard_map/fit_gather/pallas_call | solution.py:558
  125.0 196.2 %tile_exchange.1.in_ref = f32[8,104,1664]{2,1,0:T(8,128)} custom-call(f32[200,640]{1,0:T(8,128)} %get-tuple-element.7.fp_ref, f32[8,200,640]{2,1,0:T(8,128)} %get-tuple-element.8.zg_ref, f32[320,320]{1,0:T(8,128)} %l_ref.1, f32[320,320]{1,0:T(8,128)} %r_ref.1, f32[896,128]{1,0:T(8,128)} %broadcast_in_dim.18.rowd_ref, f32[8,1664]{1,0:T(8,128)} %broadcast_in_dim.20.cold_ref), custom_call_target="tpu_custom_call" | custom-call | tf_op jit(solution)/shard_map/tile_exchange/pallas_call | solution.py:602
  321.2 10.5 %lay_out.1 = f32[4000,320]{1,0:T(8,128)} custom-call(f32[8,104,1664]{2,1,0:T(8,128)} %tile_exchange.1.in_ref), custom_call_target="tpu_custom_call" | custom-call | tf_op jit(solution)/shard_map/lay_out/pallas_call | solution.py:629
  (4 shorter events, 0.0 us)

commit v4 on v3

--- a/solution.py
+++ b/solution.py
@@ -49,10 +49,10 @@
 
 def gather_kernel(
     nr, occ,
-    t_ref, b_ref, z_ref,
-    fp_ref, zg_ref,
-    tp, zp, bh, bl, sib_send, sib_recv, own, z_recv, rs_recv, zs_send, zs_recv, zc,
-    sib_s, sib_r, zz_s, zz_r, rs_s, rs_r, zs_s, zs_r, za_s, za_r, loc,
+    t_ref, b_ref, z_ref, l_ref,
+    fp_ref, zg_ref, xz_ref,
+    tp, zp, bh, bl, sib_send, sib_recv, own, z_recv, rs_recv, zs_send, zs_recv, zc, xp, xo,
+    sib_s, sib_r, zz_s, zz_r, rs_s, rs_r, zs_s, zs_r, za_s, za_r, xs, xr, loc,
 ):
     r, c = lax.axis_index("row"), lax.axis_index("col")
     t, k = c // 2, lax.rem(c, 2)
@@ -67,6 +67,10 @@
     y, low = t // 2, lax.rem(t, 2)
     pair = t + 1 - 2 * low
 
+    far = r + 1 - 2 * lax.rem(r, 2)
+    vir = va * nr
+    pad = xo.shape[0] // 2
+
     barrier = pltpu.get_barrier_semaphore()
     pl.semaphore_signal(barrier, inc=1, device_id=(r, sib), device_id_type=MESH)
 
@@ -82,12 +86,16 @@
 
         lax.fori_loop(0, count, one, 0)
 
-    each(
-        ny - 1,
-        lambda s: pl.semaphore_signal(
-            barrier, inc=1, device_id=(r, 2 * along(s) + k), device_id_type=MESH
-        ),
-    )
+    def beside(s):
+        return lax.rem(r + 2 * (s + 1), nr)
+
+    pl.semaphore_signal(barrier, inc=1, device_id=(far, c), device_id_type=MESH)
+
+    def greet(s):
+        pl.semaphore_signal(barrier, inc=1, device_id=(r, 2 * along(s) + k), device_id_type=MESH)
+        pl.semaphore_signal(barrier, inc=1, device_id=(beside(s), c), device_id_type=MESH)
+
+    each(ny - 1, greet)
 
     def greet_source(s):
         @pl.when(jnp.logical_not(jnp.logical_and(is_own, s == y)))
@@ -117,11 +125,11 @@
 
     @pl.when(is_own)
     def _():
-        pl.semaphore_wait(barrier, nr)
+        pl.semaphore_wait(barrier, nr + ny)
 
     @pl.when(jnp.logical_not(is_own))
     def _():
-        pl.semaphore_wait(barrier, nr + 1)
+        pl.semaphore_wait(barrier, nr + ny + 1)
 
     z_swap = pltpu.make_async_remote_copy(
         src_ref=zs_send, dst_ref=zs_recv, send_sem=zs_s, recv_sem=zs_r,
@@ -144,8 +152,7 @@
 
     z_push(zc, t, pair, ny - 1).start()
     each(ny - 1, lambda s: z_push(zc, t, along(s), s).start())
-    z_own = pltpu.make_async_copy(zc, zg_ref.at[t], loc)
-    z_own.start()
+    zg_ref[t] = zc[...]
 
     def to_sibling(s):
         return pltpu.make_async_remote_copy(
@@ -194,11 +201,13 @@
         def _():
             finish(s - 1)
 
+        @pl.when(s == ny)
+        def _():
+            z_push(zc, pair, pair, ny - 1).wait_recv()
+            each(ny - 1, lambda j: z_push(zg_ref.at[pair], pair, along(j), ny + j).start())
+
     each(nr, step)
     finish(nr - 1)
-
-    z_push(zc, pair, pair, ny - 1).wait_recv()
-    each(ny - 1, lambda s: z_push(zg_ref.at[pair], pair, along(s), ny + s).start())
 
     def deliver(s):
         to_pair(s).wait_recv()
@@ -213,7 +222,43 @@
         def _():
             to_owner(s).start()
 
-    each(ny, deliver)
+    def x_push(src_ref, slot, dst, sem):
+        return pltpu.make_async_remote_copy(
+            src_ref=src_ref, dst_ref=xz_ref.at[slot], send_sem=xs.at[sem], recv_sem=xr.at[slot],
+            device_id=(dst, c), device_id_type=MESH,
+        )
+
+    def deliver_early(s):
+        deliver(s)
+
+    early = ny // 2
+    each(early, deliver_early)
+
+    def z_rest(s):
+        z_push(zc, along(s), along(s), s).wait_recv()
+        z_push(zc, along(s) + pair - t, pair, s).wait_recv()
+
+    each(ny - 1, z_rest)
+    lh, ll = halves(l_ref[pl.ds(pl.multiple_of(t * va, 8), va), :])
+    xp[...] = jnp.zeros_like(xp)
+    for ii in range(og):
+        gh, gl = halves(zg_ref[:, ii * va : (ii + 1) * va, :].reshape(vir, half))
+        x = dot3(lh, ll, gh, gl, ((1,), (0,)))
+        for par in range(2):
+            for p in range(half // 128):
+                xp[p, pl.ds(par * pad + ii, vc, stride=og), :] = x[
+                    par * vc : (par + 1) * vc, p * 128 : (p + 1) * 128
+                ]
+    for p in range(half // 128):
+        xo[:, p * 128 : (p + 1) * 128] = xp[p]
+    x_push(xo, r, far, ny - 1).start()
+    each(ny - 1, lambda s: x_push(xo, r, beside(s), s).start())
+    x_own = pltpu.make_async_copy(xo, xz_ref.at[r], loc)
+    x_own.start()
+
+    each(ny - early, lambda s: deliver(early + s))
+    x_push(xo, far, far, ny - 1).wait_recv()
+    each(ny - 1, lambda s: x_push(xz_ref.at[far], far, beside(s), ny + s).start())
 
     def arrived(s):
         @pl.when(jnp.logical_not(jnp.logical_and(is_own, s == y)))
@@ -239,9 +284,11 @@
 
     def settle(s):
         z_push(zc, t, along(s), s).wait_send()
-        z_push(zc, along(s), along(s), s).wait_recv()
         z_push(zg_ref.at[pair], pair, along(s), ny + s).wait_send()
-        z_push(zc, along(s) + pair - t, pair, s).wait_recv()
+        x_push(xo, r, beside(s), s).wait_send()
+        x_push(xz_ref.at[far], far, beside(s), ny + s).wait_send()
+        x_push(xo, beside(s), far, s).wait_recv()
+        x_push(xo, lax.rem(far + 2 * (s + 1), nr), far, s).wait_recv()
 
     each(ny - 1, settle)
     each(nr, lambda s: to_sibling(s).wait_send())
@@ -254,12 +301,13 @@
             to_owner(s).wait_send()
 
     each(ny, sent)
-    z_own.wait()
+    x_push(xo, r, far, ny - 1).wait_send()
+    x_own.wait()
 
 
 def tile_kernel(
     nr, og, vc, tiles, cuts,
-    fp_ref, zg_ref, l_ref, r_ref, rowd_ref, cold_ref,
+    fp_ref, zg_ref, xz_ref, l_ref, r_ref, rowd_ref, cold_ref,
     out_ref,
     fg, rh, rl, yh, yl, xp, xo, xg, xh, xl, s_send, s_recv, own,
     fs, fr, xs, xr, ss, sr, os_, or_, loc,
@@ -270,7 +318,7 @@
     half = fp_ref.shape[1]
     vir = r_ref.shape[0]
     va = vir // nr
-    pad = xo.shape[1] // 2
+    pad = xo.shape[0] // 2
     wide_pad = xh.shape[1] // nr
     blk = lax.rem(t - r + nr, nr)
     far = r + 1 - 2 * lax.rem(r, 2)
@@ -342,26 +390,22 @@
 
         each(ny - 1, one)
 
-    for m in range(len(cuts)):
+    last = len(cuts) - 1
+    for m in range(last):
         f_start(m)
 
-    def x_cut(m):
-        return (1, 0, half) if m == len(cuts) else (0,) + cuts[m]
-
     def x_push(m, src_ref, slot, dst, sem):
         return pltpu.make_async_remote_copy(
-            src_ref=src_ref, dst_ref=xg.at[slot, x_cut(m)[0], :, pl.ds(*x_cut(m)[1:])],
+            src_ref=src_ref, dst_ref=xg.at[slot, :, pl.ds(*cuts[m])],
             send_sem=xs.at[m, sem], recv_sem=xr.at[m, slot],
             device_id=(dst, c), device_id_type=MESH,
         )
 
     def x_mine(m):
-        q, at, width = x_cut(m)
-        return xo.at[q, :, pl.ds(at, width)]
+        return xo.at[:, pl.ds(*cuts[m])]
 
     def x_far(m):
-        q, at, width = x_cut(m)
-        return xg.at[far, q, :, pl.ds(at, width)]
+        return xg.at[far, :, pl.ds(*cuts[m])]
 
     def beside(s):
         return lax.rem(r + 2 * (s + 1), nr)
@@ -377,35 +421,38 @@
         x_arrive(m, far)
         each(near, lambda s: x_push(m, x_far(m), far, beside(s), near + 1 + s).start())
 
-    def rotate(g_ref, q, at, width):
-        y_at = (1 - q) * half + at
+    def rotate(g_ref, fitted, at, width):
+        y_at = half * fitted + at
+        count = vir + va * fitted
         for ii in range(og):
             gh, gl = halves(g_ref[:, ii * va : (ii + 1) * va, at : at + width].reshape(vir, width))
-            both = dot3(rh[...], rl[...], gh, gl, ((1,), (0,)))
+            both = dot3(rh[:count], rl[:count], gh, gl, ((1,), (0,)))
             hi, lo = halves(both[:vir])
             yh[ii * vir : (ii + 1) * vir, y_at : y_at + width] = hi
             yl[ii * vir : (ii + 1) * vir, y_at : y_at + width] = lo
-            for par in range(2):
-                rows = both[vir + par * vc : vir + (par + 1) * vc]
-                for p in range(width // 128):
-                    xp[p, pl.ds(par * pad + ii, vc, stride=og), :] = rows[:, p * 128 : (p + 1) * 128]
-        for p in range(width // 128):
-            xo[q, :, at + p * 128 : at + (p + 1) * 128] = xp[p]
-
-    def take(m, src, load):
-        q, at, width = x_cut(m)
-        x_at = q * half + at
+            if fitted:
+                for par in range(2):
+                    rows = both[vir + par * vc : vir + (par + 1) * vc]
+                    for p in range(width // 128):
+                        xp[p, pl.ds(par * pad + ii, vc, stride=og), :] = rows[:, p * 128 : (p + 1) * 128]
+        if fitted:
+            for p in range(width // 128):
+                xo[:, at + p * 128 : at + (p + 1) * 128] = xp[p]
+
+    def take(src, load, x_at, width):
         rows = pl.ds(pl.multiple_of(src * wide_pad, 16), pad)
         for par in range(2):
-            hi, lo = halves(load(q, par * pad, at, width))
+            hi, lo = halves(load(par * pad))
             xh[par, rows, x_at : x_at + width] = hi
             xl[par, rows, x_at : x_at + width] = lo
 
     def take_own(m):
-        take(m, r, lambda q, row, at, width: xo[q, row : row + pad, at : at + width])
+        at, width = cuts[m]
+        take(r, lambda row: xo[row : row + pad, at : at + width], at, width)
 
     def take_from(m, src):
-        take(m, src, lambda q, row, at, width: xg[src, q, row : row + pad, at : at + width])
+        at, width = cuts[m]
+        take(src, lambda row: xg[src, row : row + pad, at : at + width], at, width)
 
     def take_near(m, base):
         def one(s):
@@ -415,19 +462,23 @@
 
         each(near, one)
 
-    zm = len(cuts)
-    rotate(zg_ref, 1, 0, half)
-    x_start(zm)
-    for m in range(zm):
-        f_forward(m)
-    order = [zm] + list(range(zm))
+    f_forward(0)
+    if last:
+        f_start(last)
+    each(nr, lambda src: take(src, lambda row: xz_ref[src, row : row + pad, :], half, half))
+    rotate(zg_ref, 0, 0, half)
+    if last > 1:
+        f_forward(1)
     for m, (at, width) in enumerate(cuts):
         f_rest(m)
-        rotate(fg, 0, at, width)
+        rotate(fg, 1, at, width)
         x_start(m)
-        x_forward(order[m])
-    x_forward(order[-1])
-    for m in order:
+        if m == 0 and last:
+            f_forward(last)
+        if m:
+            x_forward(m - 1)
+    x_forward(last)
+    for m in range(len(cuts)):
         take_own(m)
         take_from(m, far)
         take_near(m, r)
@@ -517,11 +568,11 @@
     settle(jnp.int32(tiles - 1), tail)
     to_sibling(jnp.int32(tiles - 2), WIDE).wait_send()
     to_sibling(jnp.int32(tiles - 1), tail).wait_send()
-    for m in order:
+    for m in range(len(cuts)):
         x_push(m, x_mine(m), r, far, near).wait_send()
         each(near, lambda s, m=m: x_push(m, x_mine(m), r, beside(s), s).wait_send())
         each(near, lambda s, m=m: x_push(m, x_far(m), far, beside(s), near + 1 + s).wait_send())
-    for m in range(zm):
+    for m in range(len(cuts)):
         f_push(m, fp_ref, blk, pair, ny - 1).wait_send()
         each(ny - 1, lambda s, m=m: f_push(m, fp_ref, blk, along(s), s).wait_send())
         each(ny - 1, lambda s, m=m: f_push(m, fp_ref, blk, along(s), ny + s).wait_send())
@@ -550,19 +601,22 @@
     half = naux // 2
     og, va, vc = occ // nr, vir // nr, vir // nc
     piece = og * va
+    rows = vc * og
+    pad, wide_pad = up(rows, 8), up(rows, 16)
     dma = pltpu.SemaphoreType.DMA
     vmem = pl.BlockSpec(memory_space=pltpu.VMEM)
     hbm = pl.BlockSpec(memory_space=pl.ANY)
     limit = 60 * 1024 * 1024
 
-    fp, zg = pl.pallas_call(
+    fp, zg, xz = pl.pallas_call(
         functools.partial(gather_kernel, nr, occ),
         out_shape=[
             jax.ShapeDtypeStruct((piece, half), F32),
             jax.ShapeDtypeStruct((nr, piece, half), F32),
+            jax.ShapeDtypeStruct((nr, 2 * pad, half), F32),
         ],
-        in_specs=[vmem] * 3,
-        out_specs=[vmem, hbm],
+        in_specs=[vmem] * 4,
+        out_specs=[vmem, vmem, hbm],
         scratch_shapes=[
             pltpu.VMEM((up(amplitudes.shape[1], 128) // 128, amplitudes.shape[0], 128), F32),
             pltpu.VMEM((up(naux, 128) // 128, aux_right.shape[0], 128), F32),
@@ -576,15 +630,15 @@
             pltpu.VMEM((og, vc, half), F32),
             pltpu.VMEM((og, vc, half), F32),
             pltpu.VMEM((piece, half), F32),
+            pltpu.VMEM((half // 128, 2 * pad, 128), F32),
+            pltpu.VMEM((2 * pad, half), F32),
             dma((nr,)), dma((nr,)), dma((nr,)), dma((nr,)), dma((nr,)), dma((nr,)), dma, dma,
-            dma((nr,)), dma((nr,)), dma,
+            dma((nr,)), dma((nr,)), dma((nr,)), dma((nr,)), dma,
         ],
         compiler_params=pltpu.CompilerParams(collective_id=0, has_side_effects=True, vmem_limit_bytes=limit),
         name="fit_gather",
-    )(amplitudes, aux_left, aux_right)
-
-    rows = vc * og
-    pad, wide_pad = up(rows, 8), up(rows, 16)
+    )(amplitudes, aux_left, aux_right, left_rotation)
+
     cols = og * vir
     cols_pad = up(cols, 128)
     tiles = up(cols_pad, WIDE) // WIDE
@@ -602,7 +656,7 @@
     moved = pl.pallas_call(
         functools.partial(tile_kernel, nr, og, vc, tiles, cuts),
         out_shape=jax.ShapeDtypeStruct((nr, pad, cols_pad), F32),
-        in_specs=[vmem] * 6,
+        in_specs=[vmem] * 7,
         out_specs=hbm,
         scratch_shapes=[
             pltpu.VMEM((nr, piece, half), F32),
@@ -611,20 +665,20 @@
             pltpu.VMEM((cols_pad, naux), BF16),
             pltpu.VMEM((cols_pad, naux), BF16),
             pltpu.VMEM((half // 128, 2 * pad, 128), F32),
-            pltpu.VMEM((2, 2 * pad, half), F32),
-            pltpu.VMEM((nr, 2, 2 * pad, half), F32),
+            pltpu.VMEM((2 * pad, half), F32),
+            pltpu.VMEM((nr, 2 * pad, half), F32),
             pltpu.VMEM((2, nr * wide_pad, naux), BF16),
             pltpu.VMEM((2, nr * wide_pad, naux), BF16),
             pltpu.VMEM((2, nr * wide_pad, WIDE), F32),
             pltpu.VMEM((tiles, nr * wide_pad, WIDE), F32),
             pltpu.VMEM((nr * wide_pad, cols_pad), F32),
             dma((len(cuts), nr)), dma((len(cuts), nr)),
-            dma((len(cuts) + 1, nr)), dma((len(cuts) + 1, nr)), dma((2,)), dma((tiles,)),
+            dma((len(cuts), nr)), dma((len(cuts), nr)), dma((2,)), dma((tiles,)),
             dma((tiles, nr)), dma((tiles, nr)), dma((tiles,)),
         ],
         compiler_params=pltpu.CompilerParams(collective_id=1, has_side_effects=True, vmem_limit_bytes=limit),
         name="tile_exchange",
-    )(fp, zg, left_rotation, right_rotation, rowd, cold)
+    )(fp, zg, xz, left_rotation, right_rotation, rowd, cold)
 
     out = pl.pallas_call(
         functools.partial(lay_kernel, nr, og, vir, occ),

time: 337 us -> 340 us (level)
  Pallas kernels: 320 us -> 326 us
    pallas_call x1, Pallas kernels: 113 us -> 156 us  [shards(): pl.pallas_call(functools.partial(gather_kernel, nr, occ), out_shape=[jax....]
    pallas_call x1, Pallas kernels: 196 us -> 160 us  [shards(): pl.pallas_call(functools.partial(tile_kernel, nr, og, vc, tiles, cuts), o...]
    unnamed x1 -> x5, local copies, waits for them, and re-layouts: 6.83 us -> 6.83 us
where the time goes in v4:
time: 340 us; the launch traced here: 336 us
  Pallas kernels  326 us (96%)
  local copies, waits for them, and re-layouts  9.09 us (3%)
    pallas_call x1, Pallas kernels, shards(): pl.pallas_call(functools.partial(tile_kernel, nr, og, vc, tiles, cuts), o...  160 us
    pallas_call x1, Pallas kernels, shards(): pl.pallas_call(functools.partial(gather_kernel, nr, occ), out_shape=[jax....  156 us
    pallas_call x1, Pallas kernels, shards(): pl.pallas_call(functools.partial(lay_kernel, nr, og, vir, occ), grid=(pad...  10.5 us
    unnamed x5, local copies, waits for them, and re-layouts  6.83 us

profile of v4, /device:TPU:48, one launch (start us, length us, event | category | flops | bytes accessed | tf_op | source)
XLA Modules:
  0.0 335.6 jit_solution(14520281784992111951)
XLA Ops:
  0.0 6.8 %copy.9.t_ref = f32[1600,800]{1,0:T(8,128)} copy(f32[1600,800]{0,1:T(8,128)} %param.7) | data formatting | bytes 10240000 | tf_op args[0]
  6.8 0.0 copy-start.1
  6.8 0.0 copy-start
  6.8 155.8 %fit_gather.1 = (f32[200,640]{1,0:T(8,128)}, f32[8,200,640]{2,1,0:T(8,128)}, f32[8,208,640]{2,1,0:T(8,128)}) custom-call(f32[1600,800]{1,0:T(8,128)} %copy.9.t_ref, f32[800,1280]{1,0:T(8,128)} %b_ref.1, f32[800,1280]{1,0:T(8,128)} %z_ref.1, f32[320,320]{1,0:T(8,128)} %l_ref.3), custom_call_target="tpu_custom_call" | custom-call | tf_op jit(solution)/shard_map/fit_gather/pallas_call | solution.py:611
  162.6 0.0 copy-done.1
  162.6 0.1 sub.48
  162.7 0.1 sub.50
  162.8 0.0 copy-done
  162.8 0.1 dynamic_slice.6
  162.9 0.1 sub.45
  163.0 0.1 sub.46
  163.1 0.1 broadcast_in_dim.8
  163.2 1.0 broadcast_in_dim.18.rowd_ref
  164.1 0.1 dynamic_slice.7
  164.2 0.1 broadcast_subtract_fusion
  164.3 0.1 sub.55
  164.4 0.6 broadcast_in_dim.20.cold_ref
  165.0 160.0 %tile_exchange.1.in_ref = f32[8,104,1664]{2,1,0:T(8,128)} custom-call(f32[200,640]{1,0:T(8,128)} %get-tuple-element.8.fp_ref, f32[8,200,640]{2,1,0:T(8,128)} %get-tuple-element.9.zg_ref, f32[8,208,640]{2,1,0:T(8,128)} %get-tuple-element.10.xz_ref, f32[320,320]{1,0:T(8,128)} %l_ref.3, f32[320,320]{1,0:T(8,128)} %r_ref.1, ...), custom_call_target="tpu_custom_call" | custom-call | tf_op jit(solution)/shard_map/tile_exchange/pallas_call | solution.py:656
  325.0 10.5 %lay_out.1 = f32[4000,320]{1,0:T(8,128)} custom-call(f32[8,104,1664]{2,1,0:T(8,128)} %tile_exchange.1.in_ref), custom_call_target="tpu_custom_call" | custom-call | tf_op jit(solution)/shard_map/lay_out/pallas_call | solution.py:683
  (4 shorter events, 0.0 us)
Async XLA Ops:
  6.8 155.8 %copy-start.1 = (f32[40]{0:T(128)S(1)}, f32[40]{0:T(128)}, u32[]{:S(2)}) copy-start(f32[40]{0:T(128)} %param.12) | copy-start | bytes 484
  6.8 156.0 %copy-start = (f32[320]{0:T(512)S(1)}, f32[320]{0:T(512)}, u32[]{:S(2)}) copy-start(f32[320]{0:T(512)} %param.13) | copy-start | bytes 3844

commit v5 on v4

--- a/solution.py
+++ b/solution.py
@@ -48,7 +48,7 @@
 
 
 def gather_kernel(
-    nr, occ,
+    nr, occ, zcuts,
     t_ref, b_ref, z_ref, l_ref,
     fp_ref, zg_ref, xz_ref,
     tp, zp, bh, bl, sib_send, sib_recv, own, z_recv, rs_recv, zs_send, zs_recv, zc, xp, xo,
@@ -144,14 +144,26 @@
             [jnp.where(first, z_mine, z_sib), jnp.where(first, z_sib, z_mine)], axis=0
         )
 
-    def z_push(src_ref, slot, peer, sem):
-        return pltpu.make_async_remote_copy(
-            src_ref=src_ref, dst_ref=zg_ref.at[slot], send_sem=za_s.at[sem], recv_sem=za_r.at[slot],
+    def z_push(m, src_ref, slot, peer, sem):
+        lanes = pl.ds(*zcuts[m])
+        return pltpu.make_async_remote_copy(
+            src_ref=src_ref.at[:, lanes], dst_ref=zg_ref.at[slot, :, lanes],
+            send_sem=za_s.at[m, sem], recv_sem=za_r.at[m, slot],
             device_id=(r, 2 * peer + k), device_id_type=MESH,
         )
 
-    z_push(zc, t, pair, ny - 1).start()
-    each(ny - 1, lambda s: z_push(zc, t, along(s), s).start())
+    def z_start(m):
+        z_push(m, zc, t, pair, ny - 1).start()
+        each(ny - 1, lambda s: z_push(m, zc, t, along(s), s).start())
+
+    def z_forward(m):
+        z_push(m, zc, pair, pair, ny - 1).wait_recv()
+        each(ny - 1, lambda s: z_push(m, zg_ref.at[pair], pair, along(s), ny + s).start())
+
+    def z_forwarded(m):
+        each(ny - 1, lambda s: z_push(m, zg_ref.at[pair], pair, along(s), ny + s).wait_send())
+
+    z_start(0)
     zg_ref[t] = zc[...]
 
     def to_sibling(s):
@@ -182,9 +194,13 @@
         to_sibling(s).wait_recv()
         own[s] = own[s] + sib_recv[s]
 
-        @pl.when(s < ny)
-        def _():
-            to_pair(s).start()
+        @pl.when(s == 0)
+        def _():
+            to_pair(0).start()
+
+        @pl.when(s == ny + 1)
+        def _():
+            to_pair(1).start()
 
     def step(s):
         dst = lax.rem(owner(s) - r + nr, nr)
@@ -203,11 +219,7 @@
 
         @pl.when(s == ny)
         def _():
-            z_push(zc, pair, pair, ny - 1).wait_recv()
-            each(ny - 1, lambda j: z_push(zg_ref.at[pair], pair, along(j), ny + j).start())
-
-    each(nr, step)
-    finish(nr - 1)
+            z_forward(0)
 
     def deliver(s):
         to_pair(s).wait_recv()
@@ -222,43 +234,72 @@
         def _():
             to_owner(s).start()
 
-    def x_push(src_ref, slot, dst, sem):
-        return pltpu.make_async_remote_copy(
-            src_ref=src_ref, dst_ref=xz_ref.at[slot], send_sem=xs.at[sem], recv_sem=xr.at[slot],
+    def x_push(m, src_ref, slot, dst, sem):
+        lanes = pl.ds(*zcuts[m])
+        return pltpu.make_async_remote_copy(
+            src_ref=src_ref.at[:, lanes], dst_ref=xz_ref.at[slot, :, lanes],
+            send_sem=xs.at[m, sem], recv_sem=xr.at[m, slot],
             device_id=(dst, c), device_id_type=MESH,
         )
 
-    def deliver_early(s):
-        deliver(s)
-
-    early = ny // 2
-    each(early, deliver_early)
-
-    def z_rest(s):
-        z_push(zc, along(s), along(s), s).wait_recv()
-        z_push(zc, along(s) + pair - t, pair, s).wait_recv()
-
-    each(ny - 1, z_rest)
+    def x_forward(m):
+        x_push(m, xo, far, far, ny - 1).wait_recv()
+        each(ny - 1, lambda s: x_push(m, xz_ref.at[far], far, beside(s), ny + s).start())
+
     lh, ll = halves(l_ref[pl.ds(pl.multiple_of(t * va, 8), va), :])
     xp[...] = jnp.zeros_like(xp)
-    for ii in range(og):
-        gh, gl = halves(zg_ref[:, ii * va : (ii + 1) * va, :].reshape(vir, half))
-        x = dot3(lh, ll, gh, gl, ((1,), (0,)))
-        for par in range(2):
-            for p in range(half // 128):
-                xp[p, pl.ds(par * pad + ii, vc, stride=og), :] = x[
-                    par * vc : (par + 1) * vc, p * 128 : (p + 1) * 128
-                ]
-    for p in range(half // 128):
-        xo[:, p * 128 : (p + 1) * 128] = xp[p]
-    x_push(xo, r, far, ny - 1).start()
-    each(ny - 1, lambda s: x_push(xo, r, beside(s), s).start())
+
+    def z_rows(m):
+        def z_rest(s):
+            z_push(m, zc, along(s), along(s), s).wait_recv()
+            z_push(m, zc, along(s) + pair - t, pair, s).wait_recv()
+
+        each(ny - 1, z_rest)
+        at, width = zcuts[m]
+        for ii in range(og):
+            gh, gl = halves(zg_ref[:, ii * va : (ii + 1) * va, at : at + width].reshape(vir, width))
+            x = dot3(lh, ll, gh, gl, ((1,), (0,)))
+            for par in range(2):
+                for p in range(width // 128):
+                    xp[p, pl.ds(par * pad + ii, vc, stride=og), :] = x[
+                        par * vc : (par + 1) * vc, p * 128 : (p + 1) * 128
+                    ]
+        for p in range(width // 128):
+            xo[:, at + p * 128 : at + (p + 1) * 128] = xp[p]
+        x_push(m, xo, r, far, ny - 1).start()
+        each(ny - 1, lambda s: x_push(m, xo, r, beside(s), s).start())
+
+    two = len(zcuts) > 1
+    each(nr, step)
+    finish(nr - 1)
+    deliver(0)
+    z_forwarded(0)
+    if two:
+        z_start(1)
+    to_pair(1).wait_send()
+    if ny > 2:
+        to_pair(2).start()
+    deliver(1)
+    if two:
+        z_forward(1)
+    z_rows(0)
+    for s in range(2, ny):
+        to_pair(s).wait_send()
+        if s + 1 < ny:
+            to_pair(s + 1).start()
+        deliver(s)
+        if s == 2:
+            x_forward(0)
+            if two:
+                z_rows(1)
+    if ny < 3:
+        x_forward(0)
+        if two:
+            z_rows(1)
+    if two:
+        x_forward(1)
     x_own = pltpu.make_async_copy(xo, xz_ref.at[r], loc)
     x_own.start()
-
-    each(ny - early, lambda s: deliver(early + s))
-    x_push(xo, far, far, ny - 1).wait_recv()
-    each(ny - 1, lambda s: x_push(xz_ref.at[far], far, beside(s), ny + s).start())
 
     def arrived(s):
         @pl.when(jnp.logical_not(jnp.logical_and(is_own, s == y)))
@@ -280,28 +321,29 @@
 
     lax.fori_loop(0, fp_ref.shape[0] // 8, add_up, 0)
 
-    z_push(zc, t, pair, ny - 1).wait_send()
-
-    def settle(s):
-        z_push(zc, t, along(s), s).wait_send()
-        z_push(zg_ref.at[pair], pair, along(s), ny + s).wait_send()
-        x_push(xo, r, beside(s), s).wait_send()
-        x_push(xz_ref.at[far], far, beside(s), ny + s).wait_send()
-        x_push(xo, beside(s), far, s).wait_recv()
-        x_push(xo, lax.rem(far + 2 * (s + 1), nr), far, s).wait_recv()
-
-    each(ny - 1, settle)
+    for m in range(len(zcuts)):
+        z_push(m, zc, t, pair, ny - 1).wait_send()
+        x_push(m, xo, r, far, ny - 1).wait_send()
+
+        def settle(s, m=m):
+            z_push(m, zc, t, along(s), s).wait_send()
+            x_push(m, xo, r, beside(s), s).wait_send()
+            x_push(m, xz_ref.at[far], far, beside(s), ny + s).wait_send()
+            x_push(m, xo, beside(s), far, s).wait_recv()
+            x_push(m, xo, lax.rem(far + 2 * (s + 1), nr), far, s).wait_recv()
+
+        each(ny - 1, settle)
+    if two:
+        z_forwarded(1)
     each(nr, lambda s: to_sibling(s).wait_send())
 
     def sent(s):
-        to_pair(s).wait_send()
-
         @pl.when(jnp.logical_not(jnp.logical_and(s == ny - 1, is_own)))
         def _():
             to_owner(s).wait_send()
 
+    to_pair(0).wait_send()
     each(ny, sent)
-    x_push(xo, r, far, ny - 1).wait_send()
     x_own.wait()
 
 
@@ -391,8 +433,10 @@
         each(ny - 1, one)
 
     last = len(cuts) - 1
-    for m in range(last):
-        f_start(m)
+    f_start(0)
+
+    def f_forwarded(m):
+        each(ny - 1, lambda s: f_push(m, fp_ref, blk, along(s), ny + s).wait_send())
 
     def x_push(m, src_ref, slot, dst, sem):
         return pltpu.make_async_remote_copy(
@@ -462,19 +506,18 @@
 
         each(near, one)
 
+    each(nr, lambda src: take(src, lambda row: xz_ref[src, row : row + pad, :], half, half))
     f_forward(0)
-    if last:
-        f_start(last)
-    each(nr, lambda src: take(src, lambda row: xz_ref[src, row : row + pad, :], half, half))
     rotate(zg_ref, 0, 0, half)
-    if last > 1:
-        f_forward(1)
     for m, (at, width) in enumerate(cuts):
+        f_forwarded(m)
+        if m < last:
+            f_start(m + 1)
         f_rest(m)
         rotate(fg, 1, at, width)
         x_start(m)
-        if m == 0 and last:
-            f_forward(last)
+        if m < last:
+            f_forward(m + 1)
         if m:
             x_forward(m - 1)
     x_forward(last)
@@ -575,7 +618,6 @@
     for m in range(len(cuts)):
         f_push(m, fp_ref, blk, pair, ny - 1).wait_send()
         each(ny - 1, lambda s, m=m: f_push(m, fp_ref, blk, along(s), s).wait_send())
-        each(ny - 1, lambda s, m=m: f_push(m, fp_ref, blk, along(s), ny + s).wait_send())
 
 
 def lay_kernel(nr, og, vir, occ, in_ref, out_ref, op):
@@ -608,8 +650,11 @@
     hbm = pl.BlockSpec(memory_space=pl.ANY)
     limit = 60 * 1024 * 1024
 
+    cols = og * vir
+    first = up(half * 3 // 5, 128)
+    zcuts = [(0, first), (first, half - first)] if first < half else [(0, half)]
     fp, zg, xz = pl.pallas_call(
-        functools.partial(gather_kernel, nr, occ),
+        functools.partial(gather_kernel, nr, occ, zcuts),
         out_shape=[
             jax.ShapeDtypeStruct((piece, half), F32),
             jax.ShapeDtypeStruct((nr, piece, half), F32),
@@ -633,13 +678,12 @@
             pltpu.VMEM((half // 128, 2 * pad, 128), F32),
             pltpu.VMEM((2 * pad, half), F32),
             dma((nr,)), dma((nr,)), dma((nr,)), dma((nr,)), dma((nr,)), dma((nr,)), dma, dma,
-            dma((nr,)), dma((nr,)), dma((nr,)), dma((nr,)), dma,
+            dma((2, nr)), dma((2, nr)), dma((2, nr)), dma((2, nr)), dma,
         ],
         compiler_params=pltpu.CompilerParams(collective_id=0, has_side_effects=True, vmem_limit_bytes=limit),
         name="fit_gather",
     )(amplitudes, aux_left, aux_right, left_rotation)
 
-    cols = og * vir
     cols_pad = up(cols, 128)
     tiles = up(cols_pad, WIDE) // WIDE
     cuts = [(at, min(256, half - at)) for at in range(0, half, 256)]

time: 340 us -> 327 us (0.962)
  Pallas kernels: 326 us -> 315 us
    pallas_call x1, Pallas kernels: 156 us -> 146 us  [shards(): pl.pallas_call(functools.partial(gather_kernel, nr, occ, zcuts), out_shap...]
where the time goes in v5:
time: 327 us; the launch traced here: 324 us
  Pallas kernels  315 us (96%)
  local copies, waits for them, and re-layouts  9.09 us (3%)
    pallas_call x1, Pallas kernels, shards(): pl.pallas_call(functools.partial(tile_kernel, nr, og, vc, tiles, cuts), o...  158 us
    pallas_call x1, Pallas kernels, shards(): pl.pallas_call(functools.partial(gather_kernel, nr, occ, zcuts), out_shap...  146 us
    pallas_call x1, Pallas kernels, shards(): pl.pallas_call(functools.partial(lay_kernel, nr, og, vir, occ), grid=(pad...  10.5 us
    unnamed x5, local copies, waits for them, and re-layouts  6.83 us

profile of v5, /device:TPU:48, one launch (start us, length us, event | category | flops | bytes accessed | tf_op | source)
XLA Modules:
  0.0 323.7 jit_solution(8030559140909216846)
XLA Ops:
  0.0 6.8 %copy.9.t_ref = f32[1600,800]{1,0:T(8,128)} copy(f32[1600,800]{0,1:T(8,128)} %param.7) | data formatting | bytes 10240000 | tf_op args[0]
  6.8 0.0 copy-start.1
  6.8 0.0 copy-start
  6.8 146.2 %fit_gather.1 = (f32[200,640]{1,0:T(8,128)}, f32[8,200,640]{2,1,0:T(8,128)}, f32[8,208,640]{2,1,0:T(8,128)}) custom-call(f32[1600,800]{1,0:T(8,128)} %copy.9.t_ref, f32[800,1280]{1,0:T(8,128)} %b_ref.1, f32[800,1280]{1,0:T(8,128)} %z_ref.1, f32[320,320]{1,0:T(8,128)} %l_ref.3), custom_call_target="tpu_custom_call" | custom-call | tf_op jit(solution)/shard_map/fit_gather/pallas_call | solution.py:656
  153.1 0.0 copy-done.1
  153.1 0.1 sub.48
  153.2 0.1 sub.50
  153.3 0.0 copy-done
  153.3 0.1 dynamic_slice.6
  153.4 0.1 sub.45
  153.4 0.1 sub.46
  153.5 0.1 broadcast_in_dim.8
  153.6 1.0 broadcast_in_dim.18.rowd_ref
  154.6 0.1 dynamic_slice.7
  154.7 0.1 broadcast_subtract_fusion
  154.7 0.1 sub.55
  154.8 0.6 broadcast_in_dim.20.cold_ref
  155.5 157.7 %tile_exchange.1.in_ref = f32[8,104,1664]{2,1,0:T(8,128)} custom-call(f32[200,640]{1,0:T(8,128)} %get-tuple-element.8.fp_ref, f32[8,200,640]{2,1,0:T(8,128)} %get-tuple-element.9.zg_ref, f32[8,208,640]{2,1,0:T(8,128)} %get-tuple-element.10.xz_ref, f32[320,320]{1,0:T(8,128)} %l_ref.3, f32[320,320]{1,0:T(8,128)} %r_ref.1, ...), custom_call_target="tpu_custom_call" | custom-call | tf_op jit(solution)/shard_map/tile_exchange/pallas_call | solution.py:700
  313.2 10.5 %lay_out.1 = f32[4000,320]{1,0:T(8,128)} custom-call(f32[8,104,1664]{2,1,0:T(8,128)} %tile_exchange.1.in_ref), custom_call_target="tpu_custom_call" | custom-call | tf_op jit(solution)/shard_map/lay_out/pallas_call | solution.py:727
  (4 shorter events, 0.0 us)
Async XLA Ops:
  6.8 146.2 %copy-start.1 = (f32[40]{0:T(128)S(1)}, f32[40]{0:T(128)}, u32[]{:S(2)}) copy-start(f32[40]{0:T(128)} %param.12) | copy-start | bytes 484
  6.8 146.4 %copy-start = (f32[320]{0:T(512)S(1)}, f32[320]{0:T(512)}, u32[]{:S(2)}) copy-start(f32[320]{0:T(512)} %param.13) | copy-start | bytes 3844

commit v6 on v5

--- a/solution.py
+++ b/solution.py
@@ -42,6 +42,22 @@
     lax.fori_loop(0, src.shape[0] // rows, one, 0)
 
 
+def turned(src, dst):
+    depth, width = src.shape
+    for p in range(dst.shape[0]):
+        n = min(128, depth - p * 128)
+
+        def one(g, _, p=p, n=n):
+            at = pl.ds(pl.multiple_of(g * 128, 128), 128)
+            dst[p, at, :n] = src[p * 128 : p * 128 + n, at].T
+            return 0
+
+        lax.fori_loop(0, width // 128, one, 0)
+        at = width // 128 * 128
+        if at < width:
+            dst[p, at:, :n] = src[p * 128 : p * 128 + n, at:].T
+
+
 def every(src, start, count, stride, width):
     parts = [src[p, pl.ds(start, count, stride=stride), :] for p in range(src.shape[0])]
     return jnp.concatenate(parts, axis=1)[:, :width]
@@ -51,14 +67,14 @@
     nr, occ, zcuts,
     t_ref, b_ref, z_ref, l_ref,
     fp_ref, zg_ref, xz_ref,
-    tp, zp, bh, bl, sib_send, sib_recv, own, z_recv, rs_recv, zs_send, zs_recv, zc, xp, xo,
-    sib_s, sib_r, zz_s, zz_r, rs_s, rs_r, zs_s, zs_r, za_s, za_r, xs, xr, loc,
+    tp, zp, bh, bl, sib_send, sib_recv, own, z_recv, rs_recv, fsum, zs_send, zs_recv, zc, xp, xo,
+    sib_s, sib_r, zz_s, zz_r, rs_s, rs_r, hop_s, hop_r, zs_s, zs_r, za_s, za_r, xs, xr, loc,
 ):
     r, c = lax.axis_index("row"), lax.axis_index("col")
     t, k = c // 2, lax.rem(c, 2)
     sib = c + 1 - 2 * k
     og = occ // nr
-    va = t_ref.shape[0] // occ
+    va = t_ref.shape[1] // occ
     vc = z_ref.shape[0] // occ
     half = b_ref.shape[1] // 2
     blk = lax.rem(t - r + nr, nr)
@@ -97,23 +113,11 @@
 
     each(ny - 1, greet)
 
-    def greet_source(s):
-        @pl.when(jnp.logical_not(jnp.logical_and(is_own, s == y)))
-        def _():
-            pl.semaphore_signal(
-                barrier, inc=1, device_id=(blk, 2 * (2 * s + low) + k), device_id_type=MESH
-            )
-
-    each(ny, greet_source)
-
-    planes(t_ref, tp)
+    @pl.when(jnp.logical_not(is_own))
+    def _():
+        pl.semaphore_signal(barrier, inc=1, device_id=(blk, c), device_id_type=MESH)
+
     planes(z_ref, zp)
-    mine, other = pl.ds(pl.multiple_of(k * half, half), half), pl.ds(pl.multiple_of((1 - k) * half, half), half)
-    for at, cols in ((0, other), (half, mine)):
-        hi, lo = halves(b_ref[:, cols])
-        bh[:, at : at + half] = hi
-        bl[:, at : at + half] = lo
-
     first = k == 0
     kept = []
     for jj in range(og):
@@ -125,17 +129,23 @@
 
     @pl.when(is_own)
     def _():
-        pl.semaphore_wait(barrier, nr + ny)
+        pl.semaphore_wait(barrier, nr + 1)
 
     @pl.when(jnp.logical_not(is_own))
     def _():
-        pl.semaphore_wait(barrier, nr + ny + 1)
+        pl.semaphore_wait(barrier, nr + 2)
 
     z_swap = pltpu.make_async_remote_copy(
         src_ref=zs_send, dst_ref=zs_recv, send_sem=zs_s, recv_sem=zs_r,
         device_id=(r, sib), device_id_type=MESH,
     )
     z_swap.start()
+    mine, other = pl.ds(pl.multiple_of(k * half, half), half), pl.ds(pl.multiple_of((1 - k) * half, half), half)
+    for at, cols in ((0, other), (half, mine)):
+        hi, lo = halves(b_ref[:, cols])
+        bh[:, at : at + half] = hi
+        bl[:, at : at + half] = lo
+
     z_swap.wait()
     for jj in range(og):
         z_mine = zc[jj * va : jj * va + vc, :]
@@ -165,6 +175,7 @@
 
     z_start(0)
     zg_ref[t] = zc[...]
+    turned(t_ref, tp)
 
     def to_sibling(s):
         return pltpu.make_async_remote_copy(
@@ -187,7 +198,7 @@
         ot = owner(ny + s)
         return pltpu.make_async_remote_copy(
             src_ref=own.at[ny + s], dst_ref=rs_recv.at[y], send_sem=rs_s.at[s], recv_sem=rs_r.at[y],
-            device_id=(lax.rem(ot - r + nr, nr), 2 * ot + k), device_id_type=MESH,
+            device_id=(r, 2 * ot + k), device_id_type=MESH,
         )
 
     def finish(s):
@@ -205,7 +216,7 @@
     def step(s):
         dst = lax.rem(owner(s) - r + nr, nr)
         x = jnp.concatenate(
-            [every(tp, dst * og + ii, va, occ, t_ref.shape[1]) for ii in range(og)], axis=0
+            [every(tp, dst * og + ii, va, occ, t_ref.shape[0]) for ii in range(og)], axis=0
         )
         xh, xl = halves(x)
         part = dot3(xh, xl, bh[...], bl[...], ((1,), (0,)))
@@ -224,15 +235,10 @@
     def deliver(s):
         to_pair(s).wait_recv()
         own[ny + s] = own[ny + s] + z_recv[s]
-        here = jnp.logical_and(s == ny - 1, is_own)
-
-        @pl.when(here)
-        def _():
+        if s < ny - 1:
+            to_owner(s).start()
+        else:
             rs_recv[y] = own[ny + s]
-
-        @pl.when(jnp.logical_not(here))
-        def _():
-            to_owner(s).start()
 
     def x_push(m, src_ref, slot, dst, sem):
         lanes = pl.ds(*zcuts[m])
@@ -302,24 +308,34 @@
     x_own.start()
 
     def arrived(s):
-        @pl.when(jnp.logical_not(jnp.logical_and(is_own, s == y)))
-        def _():
-            pltpu.make_async_remote_copy(
-                src_ref=own.at[0], dst_ref=rs_recv.at[s], send_sem=rs_s.at[0], recv_sem=rs_r.at[s],
-                device_id=(r, sib), device_id_type=MESH,
-            ).wait_recv()
-
-    each(ny, arrived)
-
-    def add_up(g, _):
+        pltpu.make_async_remote_copy(
+            src_ref=own.at[0], dst_ref=rs_recv.at[lax.rem(y + 1 + s, ny)], send_sem=rs_s.at[0],
+            recv_sem=rs_r.at[lax.rem(y + 1 + s, ny)],
+            device_id=(r, sib), device_id_type=MESH,
+        ).wait_recv()
+
+    each(ny - 1, arrived)
+
+    def add_up(g):
         rows = pl.ds(pl.multiple_of(g * 8, 8), 8)
         total = rs_recv[0, rows, :]
         for s in range(1, ny):
             total = total + rs_recv[s, rows, :]
-        fp_ref[rows, :] = total
-        return 0
-
-    lax.fori_loop(0, fp_ref.shape[0] // 8, add_up, 0)
+        fsum[rows, :] = total
+
+    each(fsum.shape[0] // 8, add_up)
+    hop = pltpu.make_async_remote_copy(
+        src_ref=fsum, dst_ref=fp_ref, send_sem=hop_s, recv_sem=hop_r,
+        device_id=(blk, c), device_id_type=MESH,
+    )
+
+    @pl.when(is_own)
+    def _():
+        fp_ref[...] = fsum[...]
+
+    @pl.when(jnp.logical_not(is_own))
+    def _():
+        hop.start()
 
     for m in range(len(zcuts)):
         z_push(m, zc, t, pair, ny - 1).wait_send()
@@ -337,13 +353,13 @@
         z_forwarded(1)
     each(nr, lambda s: to_sibling(s).wait_send())
 
-    def sent(s):
-        @pl.when(jnp.logical_not(jnp.logical_and(s == ny - 1, is_own)))
-        def _():
-            to_owner(s).wait_send()
+    each(ny - 1, lambda s: to_owner(s).wait_send())
+
+    @pl.when(jnp.logical_not(is_own))
+    def _():
+        hop.wait()
 
     to_pair(0).wait_send()
-    each(ny, sent)
     x_own.wait()
 
 
@@ -672,17 +688,18 @@
             pltpu.VMEM((nr, piece, half), F32),
             pltpu.VMEM((nr // 2, piece, half), F32),
             pltpu.VMEM((nr // 2, piece, half), F32),
+            pltpu.VMEM((piece, half), F32),
             pltpu.VMEM((og, vc, half), F32),
             pltpu.VMEM((og, vc, half), F32),
             pltpu.VMEM((piece, half), F32),
             pltpu.VMEM((half // 128, 2 * pad, 128), F32),
             pltpu.VMEM((2 * pad, half), F32),
-            dma((nr,)), dma((nr,)), dma((nr,)), dma((nr,)), dma((nr,)), dma((nr,)), dma, dma,
+            dma((nr,)), dma((nr,)), dma((nr,)), dma((nr,)), dma((nr,)), dma((nr,)), dma, dma, dma, dma,
             dma((2, nr)), dma((2, nr)), dma((2, nr)), dma((2, nr)), dma,
         ],
         compiler_params=pltpu.CompilerParams(collective_id=0, has_side_effects=True, vmem_limit_bytes=limit),
         name="fit_gather",
-    )(amplitudes, aux_left, aux_right, left_rotation)
+    )(amplitudes.T, aux_left, aux_right, left_rotation)
 
     cols_pad = up(cols, 128)
     tiles = up(cols_pad, WIDE) // WIDE

time: 327 us -> 294 us (0.90)
  Pallas kernels: 315 us -> 286 us
  local copies, waits for them, and re-layouts: 9.09 us -> 4.23 us
    pallas_call x1, Pallas kernels: 146 us -> 121 us  [shards(): pl.pallas_call(functools.partial(gather_kernel, nr, occ, zcuts), out_shap...]
    unnamed x5 -> x0, local copies, waits for them, and re-layouts: 6.83 us -> none
where the time goes in v6:
time: 294 us; the launch traced here: 291 us
  Pallas kernels  286 us (97%)
  local copies, waits for them, and re-layouts  4.23 us (1%)
    pallas_call x1, Pallas kernels, shards(): pl.pallas_call(functools.partial(tile_kernel, nr, og, vc, tiles, cuts), o...  155 us
    pallas_call x1, Pallas kernels, shards(): pl.pallas_call(functools.partial(gather_kernel, nr, occ, zcuts), out_shap...  121 us
    pallas_call x1, Pallas kernels, shards(): pl.pallas_call(functools.partial(lay_kernel, nr, og, vir, occ), grid=(pad...  10.5 us

profile of v6, /device:TPU:48, one launch (start us, length us, event | category | flops | bytes accessed | tf_op | source)
XLA Modules:
  0.0 291.4 jit_solution(8821549176343484257)
XLA Ops:
  0.0 0.7 dynamic_slice.7
  0.7 0.8 dynamic_slice.6
  1.5 0.7 sub.48
  2.2 0.1 sub.45
  2.3 0.1 sub.46
  2.4 0.8 broadcast_subtract_fusion
  3.1 0.1 sub.55
  3.2 0.6 broadcast_in_dim.20.cold_ref
  3.9 0.1 sub.50
  4.0 0.1 broadcast_in_dim.8
  4.1 1.0 broadcast_in_dim.18.rowd_ref
  5.0 121.1 %fit_gather.1 = (f32[200,640]{1,0:T(8,128)}, f32[8,200,640]{2,1,0:T(8,128)}, f32[8,208,640]{2,1,0:T(8,128)}) custom-call(f32[800,1600]{1,0:T(8,128)} %bitcast.2, f32[800,1280]{1,0:T(8,128)} %b_ref.1, f32[800,1280]{1,0:T(8,128)} %z_ref.1, f32[320,320]{1,0:T(8,128)} %l_ref.3), custom_call_target="tpu_custom_call" | custom-call | tf_op jit(solution)/shard_map/fit_gather/pallas_call | solution.py:672
  126.1 154.8 %tile_exchange.1.in_ref = f32[8,104,1664]{2,1,0:T(8,128)} custom-call(f32[200,640]{1,0:T(8,128)} %get-tuple-element.8.fp_ref, f32[8,200,640]{2,1,0:T(8,128)} %get-tuple-element.9.zg_ref, f32[8,208,640]{2,1,0:T(8,128)} %get-tuple-element.10.xz_ref, f32[320,320]{1,0:T(8,128)} %l_ref.3, f32[320,320]{1,0:T(8,128)} %r_ref.1, ...), custom_call_target="tpu_custom_call" | custom-call | tf_op jit(solution)/shard_map/tile_exchange/pallas_call | solution.py:717
  280.9 10.5 %lay_out.1 = f32[4000,320]{1,0:T(8,128)} custom-call(f32[8,104,1664]{2,1,0:T(8,128)} %tile_exchange.1.in_ref), custom_call_target="tpu_custom_call" | custom-call | tf_op jit(solution)/shard_map/lay_out/pallas_call | solution.py:744
  (4 shorter events, 0.0 us)

commit v7 on v6

--- a/solution.py
+++ b/solution.py
@@ -65,11 +65,15 @@
 
 def gather_kernel(
     nr, occ, zcuts,
-    t_ref, b_ref, z_ref, l_ref,
+    t_hbm, b_hbm, z_ref, l_ref,
     fp_ref, zg_ref, xz_ref,
-    tp, zp, bh, bl, sib_send, sib_recv, own, z_recv, rs_recv, fsum, zs_send, zs_recv, zc, xp, xo,
-    sib_s, sib_r, zz_s, zz_r, rs_s, rs_r, hop_s, hop_r, zs_s, zs_r, za_s, za_r, xs, xr, loc,
+    t_ref, b_ref, tp, zp, bh, bl, sib_send, sib_recv, own, z_recv, rs_recv, fsum, zs_send, zs_recv, zc, xp, xo,
+    sib_s, sib_r, zz_s, zz_r, rs_s, rs_r, hop_s, hop_r, zs_s, zs_r, za_s, za_r, xs, xr, loc, load,
 ):
+    b_load = pltpu.make_async_copy(b_hbm, b_ref, load.at[0])
+    t_load = pltpu.make_async_copy(t_hbm, t_ref, load.at[1])
+    b_load.start()
+    t_load.start()
     r, c = lax.axis_index("row"), lax.axis_index("col")
     t, k = c // 2, lax.rem(c, 2)
     sib = c + 1 - 2 * k
@@ -140,6 +144,7 @@
         device_id=(r, sib), device_id_type=MESH,
     )
     z_swap.start()
+    b_load.wait()
     mine, other = pl.ds(pl.multiple_of(k * half, half), half), pl.ds(pl.multiple_of((1 - k) * half, half), half)
     for at, cols in ((0, other), (half, mine)):
         hi, lo = halves(b_ref[:, cols])
@@ -175,6 +180,7 @@
 
     z_start(0)
     zg_ref[t] = zc[...]
+    t_load.wait()
     turned(t_ref, tp)
 
     def to_sibling(s):
@@ -365,11 +371,15 @@
 
 def tile_kernel(
     nr, og, vc, tiles, cuts,
-    fp_ref, zg_ref, xz_ref, l_ref, r_ref, rowd_ref, cold_ref,
+    fp_ref, zg_hbm, xz_hbm, l_ref, r_ref, rowd_ref, cold_ref,
     out_ref,
-    fg, rh, rl, yh, yl, xp, xo, xg, xh, xl, s_send, s_recv, own,
-    fs, fr, xs, xr, ss, sr, os_, or_, loc,
+    zg_ref, xz_ref, fg, rh, rl, yh, yl, xp, xo, xg, xh, xl, s_send, s_recv, own,
+    fs, fr, xs, xr, ss, sr, os_, or_, loc, load,
 ):
+    x_load = pltpu.make_async_copy(xz_hbm, xz_ref, load.at[0])
+    z_load = pltpu.make_async_copy(zg_hbm, zg_ref, load.at[1])
+    x_load.start()
+    z_load.start()
     r, c = lax.axis_index("row"), lax.axis_index("col")
     t, k = c // 2, lax.rem(c, 2)
     sib = c + 1 - 2 * k
@@ -394,6 +404,55 @@
 
     lax.fori_loop(0, nr - 1, greet, 0)
 
+    pl.semaphore_wait(barrier, 2 * nr - 1)
+
+    ny = nr // 2
+    y, low = t // 2, lax.rem(t, 2)
+    pair = t + 1 - 2 * low
+
+    def along(s):
+        return 2 * lax.rem(y + 1 + s, ny) + low
+
+    def slot_of(other):
+        return lax.rem(other - r + nr, nr)
+
+    def f_push(m, src_ref, slot, peer, sem):
+        at, width = cuts[m]
+        cols = pl.ds(at, width)
+        return pltpu.make_async_remote_copy(
+            src_ref=src_ref.at[:, cols], dst_ref=fg.at[slot, :, cols],
+            send_sem=fs.at[m, sem], recv_sem=fr.at[m, slot],
+            device_id=(r, 2 * peer + k), device_id_type=MESH,
+        )
+
+    def each(count, body):
+        def one(s, _):
+            body(s)
+            return 0
+
+        lax.fori_loop(0, count, one, 0)
+
+    def f_start(m):
+        f_push(m, fp_ref, blk, pair, ny - 1).start()
+        each(ny - 1, lambda s: f_push(m, fp_ref, blk, along(s), s).start())
+
+    def f_forward(m):
+        f_push(m, fp_ref, slot_of(pair), pair, ny - 1).wait_recv()
+        each(
+            ny - 1,
+            lambda s: f_push(m, fg.at[slot_of(pair)], slot_of(pair), along(s), ny + s).start(),
+        )
+
+    def f_rest(m):
+        def one(s):
+            f_push(m, fp_ref, slot_of(along(s)), pair, ny - 1).wait_recv()
+            f_push(m, fp_ref, slot_of(along(s) + pair - t), pair, ny - 1).wait_recv()
+
+        each(ny - 1, one)
+
+    last = len(cuts) - 1
+    f_start(0)
+
     hi, lo = halves(r_ref[...])
     rh[:vir, :] = hi
     rl[:vir, :] = lo
@@ -402,55 +461,6 @@
     rl[vir:, :] = lo
     xp[...] = jnp.zeros_like(xp)
     fg[blk] = fp_ref[...]
-    pl.semaphore_wait(barrier, 2 * nr - 1)
-
-    ny = nr // 2
-    y, low = t // 2, lax.rem(t, 2)
-    pair = t + 1 - 2 * low
-
-    def along(s):
-        return 2 * lax.rem(y + 1 + s, ny) + low
-
-    def slot_of(other):
-        return lax.rem(other - r + nr, nr)
-
-    def f_push(m, src_ref, slot, peer, sem):
-        at, width = cuts[m]
-        cols = pl.ds(at, width)
-        return pltpu.make_async_remote_copy(
-            src_ref=src_ref.at[:, cols], dst_ref=fg.at[slot, :, cols],
-            send_sem=fs.at[m, sem], recv_sem=fr.at[m, slot],
-            device_id=(r, 2 * peer + k), device_id_type=MESH,
-        )
-
-    def each(count, body):
-        def one(s, _):
-            body(s)
-            return 0
-
-        lax.fori_loop(0, count, one, 0)
-
-    def f_start(m):
-        f_push(m, fp_ref, blk, pair, ny - 1).start()
-        each(ny - 1, lambda s: f_push(m, fp_ref, blk, along(s), s).start())
-
-    def f_forward(m):
-        f_push(m, fp_ref, slot_of(pair), pair, ny - 1).wait_recv()
-        each(
-            ny - 1,
-            lambda s: f_push(m, fg.at[slot_of(pair)], slot_of(pair), along(s), ny + s).start(),
-        )
-
-    def f_rest(m):
-        def one(s):
-            f_push(m, fp_ref, slot_of(along(s)), pair, ny - 1).wait_recv()
-            f_push(m, fp_ref, slot_of(along(s) + pair - t), pair, ny - 1).wait_recv()
-
-        each(ny - 1, one)
-
-    last = len(cuts) - 1
-    f_start(0)
-
     def f_forwarded(m):
         each(ny - 1, lambda s: f_push(m, fp_ref, blk, along(s), ny + s).wait_send())
 
@@ -522,8 +532,10 @@
 
         each(near, one)
 
+    x_load.wait()
     each(nr, lambda src: take(src, lambda row: xz_ref[src, row : row + pad, :], half, half))
     f_forward(0)
+    z_load.wait()
     rotate(zg_ref, 0, 0, half)
     for m, (at, width) in enumerate(cuts):
         f_forwarded(m)
@@ -636,20 +648,21 @@
         each(ny - 1, lambda s, m=m: f_push(m, fp_ref, blk, along(s), s).wait_send())
 
 
-def lay_kernel(nr, og, vir, occ, in_ref, out_ref, op):
-    count, wide = op.shape[0], in_ref.shape[2]
-    for src in range(nr):
-        for jj in range(og):
-            for p in range(count):
-                start = jj * vir + p * 128
+def lay_kernel(nr, og, vir, occ, in_ref, out_ref):
+    wide = in_ref.shape[2]
+    for at in range(0, vir, 128):
+        keep = min(128, vir - at)
+        parts = []
+        for src in range(nr):
+            for jj in range(og):
+                start = jj * vir + at
                 n = min(128, wide - start)
                 v = in_ref[src, :, start : start + n]
                 if n < 128:
                     v = jnp.concatenate([v, jnp.zeros((8, 128 - n), F32)], axis=1)
-                op[p, pl.ds(src * og + jj, 8, stride=occ), :] = v
-    for p in range(count):
-        n = min(128, vir - p * 128)
-        out_ref[:, p * 128 : p * 128 + n] = op[p, :, :n]
+                parts.append(v)
+        turned_rows = jnp.swapaxes(jnp.stack(parts, axis=0), 0, 1)
+        out_ref[:, at : at + keep] = turned_rows.reshape(8 * occ, 128)[:, :keep]
 
 
 def shards(amplitudes, aux_left, aux_right, left_rotation, right_rotation, occ_energy, vir_energy):
@@ -676,9 +689,11 @@
             jax.ShapeDtypeStruct((nr, piece, half), F32),
             jax.ShapeDtypeStruct((nr, 2 * pad, half), F32),
         ],
-        in_specs=[vmem] * 4,
+        in_specs=[hbm, hbm, vmem, vmem],
         out_specs=[vmem, vmem, hbm],
         scratch_shapes=[
+            pltpu.VMEM(amplitudes.shape[::-1], F32),
+            pltpu.VMEM(aux_left.shape, F32),
             pltpu.VMEM((up(amplitudes.shape[1], 128) // 128, amplitudes.shape[0], 128), F32),
             pltpu.VMEM((up(naux, 128) // 128, aux_right.shape[0], 128), F32),
             pltpu.VMEM((aux_left.shape[0], naux), BF16),
@@ -695,7 +710,7 @@
             pltpu.VMEM((half // 128, 2 * pad, 128), F32),
             pltpu.VMEM((2 * pad, half), F32),
             dma((nr,)), dma((nr,)), dma((nr,)), dma((nr,)), dma((nr,)), dma((nr,)), dma, dma, dma, dma,
-            dma((2, nr)), dma((2, nr)), dma((2, nr)), dma((2, nr)), dma,
+            dma((2, nr)), dma((2, nr)), dma((2, nr)), dma((2, nr)), dma, dma((2,)),
         ],
         compiler_params=pltpu.CompilerParams(collective_id=0, has_side_effects=True, vmem_limit_bytes=limit),
         name="fit_gather",
@@ -717,9 +732,11 @@
     moved = pl.pallas_call(
         functools.partial(tile_kernel, nr, og, vc, tiles, cuts),
         out_shape=jax.ShapeDtypeStruct((nr, pad, cols_pad), F32),
-        in_specs=[vmem] * 7,
+        in_specs=[vmem, hbm, hbm] + [vmem] * 4,
         out_specs=hbm,
         scratch_shapes=[
+            pltpu.VMEM((nr, piece, half), F32),
+            pltpu.VMEM((nr, 2 * pad, half), F32),
             pltpu.VMEM((nr, piece, half), F32),
             pltpu.VMEM((vir + va, vir), BF16),
             pltpu.VMEM((vir + va, vir), BF16),
@@ -735,7 +752,7 @@
             pltpu.VMEM((nr * wide_pad, cols_pad), F32),
             dma((len(cuts), nr)), dma((len(cuts), nr)),
             dma((len(cuts), nr)), dma((len(cuts), nr)), dma((2,)), dma((tiles,)),
-            dma((tiles, nr)), dma((tiles, nr)), dma((tiles,)),
+            dma((tiles, nr)), dma((tiles, nr)), dma((tiles,)), dma((2,)),
         ],
         compiler_params=pltpu.CompilerParams(collective_id=1, has_side_effects=True, vmem_limit_bytes=limit),
         name="tile_exchange",
@@ -747,7 +764,6 @@
         out_shape=jax.ShapeDtypeStruct((rows * occ, vir), F32),
         in_specs=[pl.BlockSpec((nr, 8, cols_pad), lambda g: (0, g, 0))],
         out_specs=pl.BlockSpec((8 * occ, vir), lambda g: (g, 0)),
-        scratch_shapes=[pltpu.VMEM((up(vir, 128) // 128, 8 * occ, 128), F32)],
         compiler_params=pltpu.CompilerParams(vmem_limit_bytes=limit),
         name="lay_out",
     )(moved)

time: 294 us -> 290 us (0.986)
  Pallas kernels: 286 us -> 281 us
where the time goes in v7:
time: 290 us; the launch traced here: 287 us
  Pallas kernels  281 us (97%)
  local copies, waits for them, and re-layouts  4.23 us (1%)
    pallas_call x1, Pallas kernels, shards(): pl.pallas_call(functools.partial(tile_kernel, nr, og, vc, tiles, cuts), o...  153 us
    pallas_call x1, Pallas kernels, shards(): pl.pallas_call(functools.partial(gather_kernel, nr, occ, zcuts), out_shap...  118 us
    pallas_call x1, Pallas kernels, shards(): pl.pallas_call(functools.partial(lay_kernel, nr, og, vir, occ), grid=(pad...  10.4 us

profile of v7, /device:TPU:48, one launch (start us, length us, event | category | flops | bytes accessed | tf_op | source)
XLA Modules:
  0.0 286.5 jit_solution(8368044765429681087)
XLA Ops:
  0.0 0.7 dynamic_slice.7
  0.7 0.8 dynamic_slice.6
  1.5 0.7 sub.48
  2.2 0.1 sub.45
  2.3 0.1 sub.46
  2.4 0.8 broadcast_subtract_fusion
  3.1 0.1 sub.55
  3.2 0.6 broadcast_in_dim.20.cold_ref
  3.9 0.1 sub.50
  4.0 0.1 broadcast_in_dim.8
  4.1 1.0 broadcast_in_dim.18.rowd_ref
  5.0 118.4 %fit_gather.1 = (f32[200,640]{1,0:T(8,128)}, f32[8,200,640]{2,1,0:T(8,128)}, f32[8,208,640]{2,1,0:T(8,128)}) custom-call(f32[800,1600]{1,0:T(8,128)} %bitcast.2, f32[800,1280]{1,0:T(8,128)} %b_hbm.1, f32[800,1280]{1,0:T(8,128)} %z_ref.1, f32[320,320]{1,0:T(8,128)} %l_ref.3), custom_call_target="tpu_custom_call" | custom-call | tf_op jit(solution)/shard_map/fit_gather/pallas_call | solution.py:685
  123.5 152.6 %tile_exchange.1.in_ref = f32[8,104,1664]{2,1,0:T(8,128)} custom-call(f32[200,640]{1,0:T(8,128)} %get-tuple-element.8.fp_ref, f32[8,200,640]{2,1,0:T(8,128)} %get-tuple-element.9.zg_hbm, f32[8,208,640]{2,1,0:T(8,128)} %get-tuple-element.10.xz_hbm, f32[320,320]{1,0:T(8,128)} %l_ref.3, f32[320,320]{1,0:T(8,128)} %r_ref.1, ...), custom_call_target="tpu_custom_call" | custom-call | tf_op jit(solution)/shard_map/tile_exchange/pallas_call | solution.py:732
  276.1 10.4 %lay_out.1 = f32[4000,320]{1,0:T(8,128)} custom-call(f32[8,104,1664]{2,1,0:T(8,128)} %tile_exchange.1.in_ref), custom_call_target="tpu_custom_call" | custom-call | tf_op jit(solution)/shard_map/lay_out/pallas_call | solution.py:761
  (4 shorter events, 0.0 us)

commit v8 on v7

--- a/solution.py
+++ b/solution.py
@@ -650,19 +650,26 @@
 
 def lay_kernel(nr, og, vir, occ, in_ref, out_ref):
     wide = in_ref.shape[2]
-    for at in range(0, vir, 128):
-        keep = min(128, vir - at)
-        parts = []
-        for src in range(nr):
-            for jj in range(og):
-                start = jj * vir + at
-                n = min(128, wide - start)
-                v = in_ref[src, :, start : start + n]
-                if n < 128:
-                    v = jnp.concatenate([v, jnp.zeros((8, 128 - n), F32)], axis=1)
-                parts.append(v)
-        turned_rows = jnp.swapaxes(jnp.stack(parts, axis=0), 0, 1)
-        out_ref[:, at : at + keep] = turned_rows.reshape(8 * occ, 128)[:, :keep]
+
+    def group(g, _):
+        rows = pl.ds(pl.multiple_of(g * 8, 8), 8)
+        outs = pl.ds(pl.multiple_of(g * 8 * occ, 8), 8 * occ)
+        for at in range(0, vir, 128):
+            keep = min(128, vir - at)
+            parts = []
+            for src in range(nr):
+                for jj in range(og):
+                    start = jj * vir + at
+                    n = min(128, wide - start)
+                    v = in_ref[src, rows, start : start + n]
+                    if n < 128:
+                        v = jnp.concatenate([v, jnp.zeros((8, 128 - n), F32)], axis=1)
+                    parts.append(v)
+            turned_rows = jnp.swapaxes(jnp.stack(parts, axis=0), 0, 1)
+            out_ref[outs, at : at + keep] = turned_rows.reshape(8 * occ, 128)[:, :keep]
+        return 0
+
+    lax.fori_loop(0, in_ref.shape[1] // 8, group, 0)
 
 
 def shards(amplitudes, aux_left, aux_right, left_rotation, right_rotation, occ_energy, vir_energy):
@@ -760,10 +767,10 @@
 
     out = pl.pallas_call(
         functools.partial(lay_kernel, nr, og, vir, occ),
-        grid=(pad // 8,),
+        grid=(pl.cdiv(pad, 24),),
         out_shape=jax.ShapeDtypeStruct((rows * occ, vir), F32),
-        in_specs=[pl.BlockSpec((nr, 8, cols_pad), lambda g: (0, g, 0))],
-        out_specs=pl.BlockSpec((8 * occ, vir), lambda g: (g, 0)),
+        in_specs=[pl.BlockSpec((nr, 24, cols_pad), lambda g: (0, g, 0))],
+        out_specs=pl.BlockSpec((24 * occ, vir), lambda g: (g, 0)),
         compiler_params=pltpu.CompilerParams(vmem_limit_bytes=limit),
         name="lay_out",
     )(moved)

time: 290 us -> 287 us (0.990)
  Pallas kernels: 281 us -> 278 us
    pallas_call x1, Pallas kernels: 10.4 us -> 7.27 us  [shards(): pl.pallas_call(functools.partial(lay_kernel, nr, og, vir, occ), grid=(pl....]
where the time goes in v8:
time: 287 us; the launch traced here: 283 us
  Pallas kernels  278 us (97%)
  local copies, waits for them, and re-layouts  4.23 us (1%)
    pallas_call x1, Pallas kernels, shards(): pl.pallas_call(functools.partial(tile_kernel, nr, og, vc, tiles, cuts), o...  153 us
    pallas_call x1, Pallas kernels, shards(): pl.pallas_call(functools.partial(gather_kernel, nr, occ, zcuts), out_shap...  118 us
    pallas_call x1, Pallas kernels, shards(): pl.pallas_call(functools.partial(lay_kernel, nr, og, vir, occ), grid=(pl....  7.27 us

profile of v8, /device:TPU:48, one launch (start us, length us, event | category | flops | bytes accessed | tf_op | source)
XLA Modules:
  0.0 283.4 jit_solution(10733304893441881538)
XLA Ops:
  0.0 0.7 dynamic_slice.7
  0.7 0.8 dynamic_slice.6
  1.5 0.7 sub.48
  2.2 0.1 sub.45
  2.3 0.1 sub.46
  2.4 0.8 broadcast_subtract_fusion
  3.1 0.1 sub.55
  3.2 0.6 broadcast_in_dim.20.cold_ref
  3.9 0.1 sub.50
  4.0 0.1 broadcast_in_dim.8
  4.1 1.0 broadcast_in_dim.18.rowd_ref
  5.0 118.4 %fit_gather.1 = (f32[200,640]{1,0:T(8,128)}, f32[8,200,640]{2,1,0:T(8,128)}, f32[8,208,640]{2,1,0:T(8,128)}) custom-call(f32[800,1600]{1,0:T(8,128)} %bitcast.2, f32[800,1280]{1,0:T(8,128)} %b_hbm.1, f32[800,1280]{1,0:T(8,128)} %z_ref.1, f32[320,320]{1,0:T(8,128)} %l_ref.3), custom_call_target="tpu_custom_call" | custom-call | tf_op jit(solution)/shard_map/fit_gather/pallas_call | solution.py:692
  123.5 152.6 %tile_exchange.1.in_ref = f32[8,104,1664]{2,1,0:T(8,128)} custom-call(f32[200,640]{1,0:T(8,128)} %get-tuple-element.8.fp_ref, f32[8,200,640]{2,1,0:T(8,128)} %get-tuple-element.9.zg_hbm, f32[8,208,640]{2,1,0:T(8,128)} %get-tuple-element.10.xz_hbm, f32[320,320]{1,0:T(8,128)} %l_ref.3, f32[320,320]{1,0:T(8,128)} %r_ref.1, ...), custom_call_target="tpu_custom_call" | custom-call | tf_op jit(solution)/shard_map/tile_exchange/pallas_call | solution.py:739
  276.1 7.3 %lay_out.1 = f32[4000,320]{1,0:T(8,128)} custom-call(f32[8,104,1664]{2,1,0:T(8,128)} %tile_exchange.1.in_ref), custom_call_target="tpu_custom_call" | custom-call | tf_op jit(solution)/shard_map/lay_out/pallas_call | solution.py:768
  (4 shorter events, 0.0 us)
